TPU v7x, 32 devices: a whole 2x2x4 slice. The times are simulated.
32 devices in a mesh: ctx: 16 (over z, x, core), tp: 2 (over y).
Axes of the slice: x: 2, y: 2, z: 4, core: 2. Of those that a mesh axis runs over, the one named last changes fastest.
Arguments:
- query: bfloat16 [2048, 4096], P('ctx', 'tp'), as said below
- key_proj: bfloat16 [2048, 4096], P('ctx', 'tp'), may hold values from -6 to 6
- value_proj: bfloat16 [2048, 4096], P('ctx', 'tp'), may hold values from -6 to 6
- filter_taps: bfloat16 [2048, 4096], P('ctx', 'tp'), may hold values from -6 to 6
- grad_out: bfloat16 [2048, 4096], P('ctx', 'tp'), may hold values from -6 to 6
Outputs:
- mixer_out: bfloat16 [2048, 4096], P('ctx', 'tp')
- dquery: bfloat16 [2048, 4096], P('ctx', 'tp')
- dkey: bfloat16 [2048, 4096], P('ctx', 'tp')
- dvalue: bfloat16 [2048, 4096], P('ctx', 'tp')
- dtaps: bfloat16 [2048, 4096], P('ctx', 'tp')
Inputs may be any that keep to these rules, and one draw needn't show every extreme that they name: Entries of query are real values of either sign.
All inputs are finite; a program needn't handle non-finite values.
Results may differ from a plain program's by a relative error of at most 0.0085.
Values may be sent and summed in bfloat16 or wider, within the bound.
No kernel may reach another device: no remote copies, remote signals or barrier semaphores. Data moves between devices by JAX's collectives and lax.ppermute only.
A program may use at most 64 MiB of HBM per device.

v0:
```python
import math

import jax
import jax.numpy as jnp
from jax import lax
from jax.sharding import PartitionSpec as P

precise = lax.Precision.HIGHEST


def dft_tables(size_count):
    index = jnp.arange(size_count, dtype=jnp.int32)
    angle = (
        2.0
        * math.pi
        / size_count
        * (index[:, None] * index[None, :] % size_count).astype(jnp.float32)
    )
    return (jnp.cos(angle), jnp.sin(angle))


def twiddles(row_count, col_count):
    total = row_count * col_count
    row_index = jnp.arange(row_count, dtype=jnp.int32)
    col_index = jnp.arange(col_count, dtype=jnp.int32)
    angle = (
        2.0
        * math.pi
        / total
        * (row_index[:, None] * col_index[None, :] % total).astype(jnp.float32)
    )
    return (jnp.cos(angle), jnp.sin(angle))


def left_apply(table, blocks):
    return jnp.einsum("ka,cab->ckb", table, blocks, precision=precise)


def right_apply(blocks, table):
    return jnp.einsum("cka,ab->ckb", blocks, table, precision=precise)


def spectrum(signal):
    channels, length = signal.shape
    total = 2 * length
    row_count = 128
    col_count = total // row_count
    padded = jnp.concatenate(
        [signal.astype(jnp.float32), jnp.zeros((channels, length), jnp.float32)], axis=1
    )
    padded = padded.reshape(channels, row_count, col_count)
    cos_rows, sin_rows = dft_tables(row_count)
    cos_cols, sin_cols = dft_tables(col_count)
    cos_twist, sin_twist = twiddles(row_count, col_count)
    first_real = left_apply(cos_rows, padded)
    first_imag = -left_apply(sin_rows, padded)
    turned_real = first_real * cos_twist + first_imag * sin_twist
    turned_imag = first_imag * cos_twist - first_real * sin_twist
    spec_real = right_apply(turned_real, cos_cols) + right_apply(turned_imag, sin_cols)
    spec_imag = right_apply(turned_imag, cos_cols) - right_apply(turned_real, sin_cols)
    return (spec_real, spec_imag)


def signal_of(spec_real, spec_imag, length):
    channels, row_count, col_count = spec_real.shape
    total = row_count * col_count
    cos_rows, sin_rows = dft_tables(row_count)
    cos_cols, sin_cols = dft_tables(col_count)
    cos_twist, sin_twist = twiddles(row_count, col_count)
    back_real = right_apply(spec_real, cos_cols) - right_apply(spec_imag, sin_cols)
    back_imag = right_apply(spec_imag, cos_cols) + right_apply(spec_real, sin_cols)
    turned_real = back_real * cos_twist - back_imag * sin_twist
    turned_imag = back_imag * cos_twist + back_real * sin_twist
    values = left_apply(cos_rows, turned_real) - left_apply(sin_rows, turned_imag)
    return values.reshape(channels, total)[:, :length] / total


def times_plain(left_real, left_imag, right_real, right_imag):
    return (
        left_real * right_real - left_imag * right_imag,
        left_real * right_imag + left_imag * right_real,
    )


def times_conj(left_real, left_imag, right_real, right_imag):
    return (
        left_real * right_real + left_imag * right_imag,
        left_imag * right_real - left_real * right_imag,
    )


def channel_total(values):
    return lax.psum(values, "tp")


def per_device(query, key_proj, value_proj, filter_taps, grad_out):
    length = query.shape[0] * lax.axis_size("ctx")
    width = query.shape[1] * lax.axis_size("tp")
    filter_scale = 1.0 / math.sqrt(length)
    mixed_rows = (key_proj.astype(jnp.float32) * value_proj.astype(jnp.float32)).astype(
        jnp.bfloat16
    )
    mixed_cols, taps_cols = (
        lax.all_to_all(mixed_rows.T, "ctx", split_axis=0, concat_axis=1, tiled=True),
        lax.all_to_all(filter_taps.T, "ctx", split_axis=0, concat_axis=1, tiled=True),
    )
    taps_real, taps_imag = spectrum(taps_cols)
    mixed_real, mixed_imag = spectrum(mixed_cols)
    conv_real, conv_imag = times_plain(mixed_real, mixed_imag, taps_real, taps_imag)
    conv_cols = (filter_scale * signal_of(conv_real, conv_imag, length)).astype(jnp.bfloat16)
    conv_rows = lax.all_to_all(conv_cols, "ctx", split_axis=1, concat_axis=0, tiled=True).T
    conv_float = conv_rows.astype(jnp.float32)
    query_float = query.astype(jnp.float32)
    gated = query_float * conv_float
    upstream = grad_out.astype(jnp.float32)
    square_sum = channel_total(jnp.sum(gated * gated, axis=1))
    inverse_rms = lax.rsqrt(square_sum / width + 1e-05)
    mixer_out = (gated * inverse_rms[:, None]).astype(jnp.bfloat16)
    dots = channel_total(jnp.sum(upstream * gated, axis=1)) / width
    dgated = inverse_rms[:, None] * upstream - (inverse_rms**3 * dots)[:, None] * gated
    dquery = (dgated * conv_float).astype(jnp.bfloat16)
    gconv = (dgated * query_float).astype(jnp.bfloat16)
    grad_cols = lax.all_to_all(gconv.T, "ctx", split_axis=0, concat_axis=1, tiled=True)
    grad_real, grad_imag = spectrum(grad_cols)
    back_real, back_imag = times_conj(grad_real, grad_imag, taps_real, taps_imag)
    dmixed_cols = (filter_scale * signal_of(back_real, back_imag, length)).astype(jnp.bfloat16)
    tap_real, tap_imag = times_conj(grad_real, grad_imag, mixed_real, mixed_imag)
    dtaps_cols = (filter_scale * signal_of(tap_real, tap_imag, length)).astype(jnp.bfloat16)
    dmixed_back, dtaps_back = (
        lax.all_to_all(dmixed_cols, "ctx", split_axis=1, concat_axis=0, tiled=True),
        lax.all_to_all(dtaps_cols, "ctx", split_axis=1, concat_axis=0, tiled=True),
    )
    dmixed_float = dmixed_back.T.astype(jnp.float32)
    dkey = (dmixed_float * value_proj.astype(jnp.float32)).astype(jnp.bfloat16)
    dvalue = (dmixed_float * key_proj.astype(jnp.float32)).astype(jnp.bfloat16)
    dtaps = dtaps_back.T
    return (mixer_out, dquery, dkey, dvalue, dtaps)


def solution(mesh):
    in_specs = (P("ctx", "tp"), P("ctx", "tp"), P("ctx", "tp"), P("ctx", "tp"), P("ctx", "tp"))
    out_specs = (P("ctx", "tp"), P("ctx", "tp"), P("ctx", "tp"), P("ctx", "tp"), P("ctx", "tp"))
    return jax.shard_map(
        per_device, mesh=mesh, in_specs=in_specs, out_specs=out_specs, check_vma=False
    )
```

profile of v0, /device:TPU:1, one launch (start us, length us, event | category | flops | bytes accessed | tf_op | source)
XLA Modules:
  0.0 273.2 jit_solution(9572580252091926865)
XLA Ops:
  4.5 7.3 %all-to-all-start = ((bf16[16,128,128]{2,1,0:T(8,128)(2,1)}), bf16[16,128,128]{2,1,0:T(8,128)(2,1)S(1)}, u32[]{:S(2)}, u32[]{:S(2)}) async-start(bf16[16,128,128]{2,1,0:T(8,128)(2,1)} %bitcast.1), calls=%async_computation | async-start | bytes 1048576 | tf_op jit(solution)/shard_map/all_to_all | solution.py:104
  12.8 13.0 %all-to-all-done = bf16[16,128,128]{2,1,0:T(8,128)(2,1)S(1)} async-done(((bf16[16,128,128]{2,1,0:T(8,128)(2,1)}), bf16[16,128,128]{2,1,0:T(8,128)(2,1)S(1)}, u32[]{:S(2)}, u32[]{:S(2)}) %all-to-all-start) | async-done | bytes 524320 | tf_op jit(solution)/shard_map/all_to_all | solution.py:104
  25.8 4.4 %all-to-all-start.1 = ((bf16[16,128,128]{2,1,0:T(8,128)(2,1)}), bf16[16,128,128]{2,1,0:T(8,128)(2,1)}, u32[]{:S(2)}, u32[]{:S(2)}) async-start(bf16[16,128,128]{2,1,0:T(8,128)(2,1)} %bitcast.12), calls=%async_computation.1 | async-start | bytes 1048576 | tf_op jit(solution)/shard_map/all_to_all | solution.py:105
  35.5 8.8 %all-to-all-done.1 = bf16[16,128,128]{2,1,0:T(8,128)(2,1)} async-done(((bf16[16,128,128]{2,1,0:T(8,128)(2,1)}), bf16[16,128,128]{2,1,0:T(8,128)(2,1)}, u32[]{:S(2)}, u32[]{:S(2)}) %all-to-all-start.1) | async-done | bytes 524320 | tf_op jit(solution)/shard_map/all_to_all | solution.py:105
  59.5 3.4 %fusion.48 = f32[128,128,32]{1,2,0:T(8,128)S(1)} fusion(f32[128,128,32]{1,0,2:T(8,128)S(1)} %get-tuple-element.33), kind=kOutput, calls=%fused_computation.75 | convolution fusion | flops 201340928 | bytes 4194304 | tf_op jit(solution)/shard_map/cka,ab->ckb/dot_general | solution.py:40
  66.2 3.3 %fusion.60 = f32[128,128,32]{1,2,0:T(8,128)S(1)} fusion(f32[128,128,32]{1,2,0:T(8,128)S(1)} %fusion.40, f32[128,128,32]{1,0,2:T(8,128)S(1)} %get-tuple-element.22), kind=kOutput, calls=%fused_computation.83 | convolution fusion | flops 201865216 | bytes 6291456 | tf_op jit(solution)/shard_map/cka,ab->ckb/dot_general | solution.py:40
  72.8 3.5 %fusion.54 = f32[128,128,32]{1,2,0:T(8,128)S(1)} fusion(f32[128,128,32]{1,2,0:T(8,128)S(1)} %fusion.48, f32[128,128,32]{1,0,2:T(8,128)S(1)} %get-tuple-element.34), kind=kOutput, calls=%fused_computation.81 | convolution fusion | flops 201865216 | bytes 6291456 | tf_op jit(solution)/shard_map/cka,ab->ckb/dot_general | solution.py:40
  76.4 5.3 %multiply_subtract_fusion.2 = (f32[128,128,32]{1,2,0:T(8,128)S(1)}, f32[128,128,32]{1,2,0:T(8,128)S(1)}, f32[128,128,32]{1,2,0:T(8,128)}) fusion(f32[128,128,32]{1,2,0:T(8,128)S(1)} %fusion.63, f32[128,128,32]{1,2,0:T(8,128)S(1)} %fusion.54, f32[128,128,32]{1,2,0:T(8,128)S(1)} %fusion.60, f32[128,128,32]{1,2,0:T(8,128)S(1)} %fusion.46, ...), kind=kOutput, calls=%fused_computation.56 | convolution fusion | flops 205010944 | bytes 16777216 | tf_op jit(solution)/shard_map/cka,ab->ckb/dot_general | solution.py:40
  90.1 9.2 %fusion.22 = f32[128,32,128]{0,2,1:T(8,128)S(1)} fusion(f32[128,32]{0,1:T(8,128)S(1)} %get-tuple-element.38, f32[128,32]{0,1:T(8,128)S(1)} %get-tuple-element.39, f32[128,128,32]{1,2,0:T(8,128)S(1)} %fusion.156, f32[128,128,32]{1,2,0:T(8,128)S(1)} %fusion.174, f32[128,128,32]{1,2,0:T(8,128)S(1)} %fusion.154, f32[128,128,32]{1,2,0:T(8,128)S(1)} %fusion.172), kind=kOutput, calls=%fused_computation.47 | convolution fusion | flops 808157184 | bytes 10518528 | tf_op jit(solution)/shard_map/ka,cab->ckb/dot_general | solution.py:36
  99.3 9.5 %subtract_bitcast_fusion.2 = f32[128,128,32]{0,1,2:T(8,128)S(1)} fusion(f32[128,32,128]{0,2,1:T(8,128)S(1)} %fusion.22, f32[128,32]{0,1:T(8,128)S(1)} %get-tuple-element.38, f32[128,32]{0,1:T(8,128)S(1)} %get-tuple-element.39, f32[128,128,32]{1,2,0:T(8,128)S(1)} %fusion.156, f32[128,128,32]{1,2,0:T(8,128)S(1)} %fusion.174, ...), kind=kOutput, calls=%fused_computation.46 | convolution fusion | flops 808681472 | bytes 12615680 | tf_op jit(solution)/shard_map/ka,cab->ckb/dot_general | solution.py:36
  111.0 4.4 %all-to-all-start.2 = ((bf16[128,16,128]{0,2,1:T(8,128)(2,1)}), bf16[128,16,128]{0,2,1:T(8,128)(2,1)S(1)}, u32[]{:S(2)}, u32[]{:S(2)}) async-start(bf16[128,16,128]{0,2,1:T(8,128)(2,1)} %bitcast.20), calls=%async_computation.2 | async-start | bytes 1048576 | tf_op jit(solution)/shard_map/all_to_all | solution.py:111
  118.5 11.0 %all-to-all-done.2 = bf16[128,16,128]{0,2,1:T(8,128)(2,1)S(1)} async-done(((bf16[128,16,128]{0,2,1:T(8,128)(2,1)}), bf16[128,16,128]{0,2,1:T(8,128)(2,1)S(1)}, u32[]{:S(2)}, u32[]{:S(2)}) %all-to-all-start.2) | async-done | bytes 524320 | tf_op jit(solution)/shard_map/all_to_all | solution.py:111
  133.6 3.8 %all-reduce.3 = (f32[128]{0:T(128)S(1)}, f32[128]{0:T(128)S(1)}) all-reduce(f32[128]{0:T(128)S(1)} %get-tuple-element.11, f32[128]{0:T(128)S(1)} %get-tuple-element.10), channel_id=1, replica_groups=mesh['ctx'=16,'tp'=2] {'tp'}, use_global_device_ids=true, to_apply=%region_1.2 | all-reduce | flops 256 | bytes 2048 | tf_op jit(solution)/shard_map/psum | solution.py:93
  139.9 19.4 %all_to_all.84 = bf16[16,128,128]{2,1,0:T(8,128)(2,1)S(1)} all-to-all(bf16[16,128,128]{2,1,0:T(8,128)(2,1)S(1)} %bitcast.217), channel_id=1, replica_groups=mesh['ctx'=16,'tp'=2] {'ctx'}, dimensions={0} | all-to-all | bytes 1048576 | tf_op jit(solution)/shard_map/all_to_all | solution.py:123
  172.3 3.6 %fusion.66 = f32[128,128,32]{1,2,0:T(8,128)S(1)} fusion(f32[128,128,32]{1,2,0:T(8,128)S(1)} %fusion.32, f32[128,128,32]{1,0,2:T(8,128)S(1)} %get-tuple-element.20), kind=kOutput, calls=%fused_computation.85 | convolution fusion | flops 201865216 | bytes 6291456 | tf_op jit(solution)/shard_map/cka,ab->ckb/dot_general | solution.py:40
  175.9 4.5 %multiply_add_fusion = (f32[128,128,32]{1,2,0:T(8,128)S(1)}, f32[128,128,32]{1,2,0:T(8,128)S(1)}, f32[128,128,32]{1,2,0:T(8,128)S(1)}, f32[128,128,32]{1,2,0:T(8,128)S(1)}) fusion(f32[128,128,32]{1,2,0:T(8,128)S(1)} %copy-done.8, f32[128,128,32]{1,2,0:T(8,128)S(1)} %fusion.66, f32[128,128,32]{1,2,0:T(8,128)S(1)} %copy-done.6, ...), kind=kOutput, calls=%fused_computation.34 | convolution fusion | flops 208156672 | bytes 23068672 | tf_op jit(solution)/shard_map/cka,ab->ckb/dot_general | solution.py:40
  190.6 3.3 %fusion.166 = f32[128,128,32]{1,2,0:T(8,128)} fusion(f32[128,128,32]{1,2,0:T(8,128)S(1)} %get-tuple-element.26), kind=kOutput, calls=%fused_computation.187 | convolution fusion | flops 201340928 | bytes 4194304 | tf_op jit(solution)/shard_map/cka,ab->ckb/dot_general | solution.py:40
  200.5 9.7 %fusion.6 = f32[128,32,128]{0,2,1:T(8,128)S(1)} fusion(f32[128,32]{0,1:T(8,128)S(1)} %get-tuple-element.38, f32[128,32]{0,1:T(8,128)S(1)} %get-tuple-element.39, f32[128,128,32]{1,2,0:T(8,128)S(1)} %fusion.146, f32[128,128,32]{1,2,0:T(8,128)S(1)} %fusion.164, f32[128,128,32]{1,2,0:T(8,128)S(1)} %fusion.144, f32[128,128,32]{1,2,0:T(8,128)S(1)} %fusion.162), kind=kOutput, calls=%fused_computation.25 | convolution fusion | flops 808157184 | bytes 10518528 | tf_op jit(solution)/shard_map/ka,cab->ckb/dot_general | solution.py:36
  210.2 10.1 %subtract_bitcast_fusion = f32[128,128,32]{0,1,2:T(8,128)S(1)} fusion(f32[128,32,128]{0,2,1:T(8,128)S(1)} %fusion.6, f32[128,32]{0,1:T(8,128)S(1)} %get-tuple-element.38, f32[128,32]{0,1:T(8,128)S(1)} %get-tuple-element.39, f32[128,128,32]{1,2,0:T(8,128)S(1)} %fusion.146, f32[128,128,32]{1,2,0:T(8,128)S(1)} %fusion.164, f32[128,128,32]{1,2,0:T(8,128)S(1)} %fusion.144, ...), kind=kOutput, calls=%fused_computation.24 | convolution fusion | flops 808681472 | bytes 12615680 | tf_op jit(solution)/shard_map/ka,cab->ckb/dot_general | solution.py:36
  222.4 4.5 %all-to-all-start.5 = ((bf16[128,16,128]{0,2,1:T(8,128)(2,1)}), bf16[128,16,128]{0,2,1:T(8,128)(2,1)S(1)}, u32[]{:S(2)}, u32[]{:S(2)}) async-start(bf16[128,16,128]{0,2,1:T(8,128)(2,1)} %bitcast.41), calls=%async_computation.5 | async-start | bytes 1048576 | tf_op jit(solution)/shard_map/all_to_all | solution.py:131
  226.9 11.8 %fusion.14 = f32[128,32,128]{0,2,1:T(8,128)S(1)} fusion(f32[128,32]{0,1:T(8,128)S(1)} %get-tuple-element.38, f32[128,32]{0,1:T(8,128)S(1)} %get-tuple-element.39, f32[128,128,32]{1,2,0:T(8,128)S(1)} %fusion.150, f32[128,128,32]{1,2,0:T(8,128)} %fusion.168, f32[128,128,32]{1,2,0:T(8,128)} %fusion.148, f32[128,128,32]{1,2,0:T(8,128)} %fusion.166), kind=kOutput, calls=%fused_computation.36 | convolution fusion | flops 808157184 | bytes 10518528 | tf_op jit(solution)/shard_map/ka,cab->ckb/dot_general | solution.py:36
  238.7 9.4 %subtract_bitcast_fusion.1 = f32[128,128,32]{0,1,2:T(8,128)S(1)} fusion(f32[128,32,128]{0,2,1:T(8,128)S(1)} %fusion.14, f32[128,32]{0,1:T(8,128)S(1)} %get-tuple-element.38, f32[128,32]{0,1:T(8,128)S(1)} %get-tuple-element.39, f32[128,128,32]{1,2,0:T(8,128)S(1)} %fusion.150, f32[128,128,32]{1,2,0:T(8,128)S(1)} %copy-done.2, ...), kind=kOutput, calls=%fused_computation.35 | convolution fusion | flops 808681472 | bytes 12615680 | tf_op jit(solution)/shard_map/ka,cab->ckb/dot_general | solution.py:36
  250.2 6.0 %all-to-all-start.4 = ((bf16[128,16,128]{0,2,1:T(8,128)(2,1)}), bf16[128,16,128]{0,2,1:T(8,128)(2,1)S(1)}, u32[]{:S(2)}, u32[]{:S(2)}) async-start(bf16[128,16,128]{0,2,1:T(8,128)(2,1)} %bitcast.34), calls=%async_computation.4 | async-start | bytes 1048576 | tf_op jit(solution)/shard_map/all_to_all | solution.py:130
  260.6 9.7 %all-to-all-done.4 = bf16[128,16,128]{0,2,1:T(8,128)(2,1)S(1)} async-done(((bf16[128,16,128]{0,2,1:T(8,128)(2,1)}), bf16[128,16,128]{0,2,1:T(8,128)(2,1)S(1)}, u32[]{:S(2)}, u32[]{:S(2)}) %all-to-all-start.4) | async-done | bytes 524320 | tf_op jit(solution)/shard_map/all_to_all | solution.py:130
  (92 shorter events, 92.9 us)
Async XLA Ops:
  1.9 10.8 %copy-start.9 = (bf16[128,2048]{0,1:T(8,128)(2,1)}, bf16[128,2048]{0,1:T(8,128)(2,1)S(1)}, u32[]{:S(2)}) copy-start(bf16[128,2048]{0,1:T(8,128)(2,1)S(1)} %copy.68) | copy-start | bytes 1572868
  2.0 9.8 %copy-start.14 = (bf16[128,2048]{1,0:T(8,128)(2,1)S(1)}, bf16[128,2048]{1,0:T(8,128)(2,1)}, u32[]{:S(2)}) copy-start(bf16[128,2048]{1,0:T(8,128)(2,1)} %param.8) | copy-start | bytes 1572868
  3.5 22.3 %copy-start.11 = (bf16[128,2048]{0,1:T(8,128)(2,1)}, bf16[128,2048]{0,1:T(8,128)(2,1)S(1)}, u32[]{:S(2)}) copy-start(bf16[128,2048]{0,1:T(8,128)(2,1)S(1)} %copy.69) | copy-start | bytes 1572868
  4.5 21.3 %all-to-all-start = ((bf16[16,128,128]{2,1,0:T(8,128)(2,1)}), bf16[16,128,128]{2,1,0:T(8,128)(2,1)S(1)}, u32[]{:S(2)}, u32[]{:S(2)}) async-start(bf16[16,128,128]{2,1,0:T(8,128)(2,1)} %bitcast.1), calls=%async_computation | async-start | bytes 1048576 | tf_op jit(solution)/shard_map/all_to_all | solution.py:104
  25.8 18.5 %all-to-all-start.1 = ((bf16[16,128,128]{2,1,0:T(8,128)(2,1)}), bf16[16,128,128]{2,1,0:T(8,128)(2,1)}, u32[]{:S(2)}, u32[]{:S(2)}) async-start(bf16[16,128,128]{2,1,0:T(8,128)(2,1)} %bitcast.12), calls=%async_computation.1 | async-start | bytes 1048576 | tf_op jit(solution)/shard_map/all_to_all | solution.py:105
  49.2 1.6 copy-start.7
  72.8 3.6 %copy-start.3 = (f32[128,128,32]{1,2,0:T(8,128)}, f32[128,128,32]{1,2,0:T(8,128)S(1)}, u32[]{:S(2)}) copy-start(f32[128,128,32]{1,2,0:T(8,128)S(1)} %fusion.63) | copy-start | bytes 6291460
  76.4 5.3 %copy-start.5 = (f32[128,128,32]{1,2,0:T(8,128)}, f32[128,128,32]{1,2,0:T(8,128)S(1)}, u32[]{:S(2)}) copy-start(f32[128,128,32]{1,2,0:T(8,128)S(1)} %fusion.54) | copy-start | bytes 6291460
  110.1 5.3 %copy-start.15 = (bf16[128,2048]{1,0:T(8,128)(2,1)S(1)}, bf16[128,2048]{1,0:T(8,128)(2,1)}, u32[]{:S(2)}) copy-start(bf16[128,2048]{1,0:T(8,128)(2,1)} %param.5) | copy-start | bytes 1572868
  111.0 18.4 %all-to-all-start.2 = ((bf16[128,16,128]{0,2,1:T(8,128)(2,1)}), bf16[128,16,128]{0,2,1:T(8,128)(2,1)S(1)}, u32[]{:S(2)}, u32[]{:S(2)}) async-start(bf16[128,16,128]{0,2,1:T(8,128)(2,1)} %bitcast.20), calls=%async_computation.2 | async-start | bytes 1048576 | tf_op jit(solution)/shard_map/all_to_all | solution.py:111
  172.2 3.6 %copy-start.4 = (f32[128,128,32]{1,2,0:T(8,128)S(1)}, f32[128,128,32]{1,2,0:T(8,128)}, u32[]{:S(2)}) copy-start(f32[128,128,32]{1,2,0:T(8,128)} %copy-done.3) | copy-start | bytes 6291460
  172.2 3.6 %copy-start.6 = (f32[128,128,32]{1,2,0:T(8,128)S(1)}, f32[128,128,32]{1,2,0:T(8,128)}, u32[]{:S(2)}) copy-start(f32[128,128,32]{1,2,0:T(8,128)} %copy-done.5) | copy-start | bytes 6291460
  172.3 3.6 %copy-start.8 = (f32[128,128,32]{1,2,0:T(8,128)S(1)}, f32[128,128,32]{1,2,0:T(8,128)}, u32[]{:S(2)}) copy-start(f32[128,128,32]{1,2,0:T(8,128)} %get-tuple-element.37) | copy-start | bytes 6291460
  222.4 27.8 %all-to-all-start.5 = ((bf16[128,16,128]{0,2,1:T(8,128)(2,1)}), bf16[128,16,128]{0,2,1:T(8,128)(2,1)S(1)}, u32[]{:S(2)}, u32[]{:S(2)}) async-start(bf16[128,16,128]{0,2,1:T(8,128)(2,1)} %bitcast.41), calls=%async_computation.5 | async-start | bytes 1048576 | tf_op jit(solution)/shard_map/all_to_all | solution.py:131
  226.8 11.8 %copy-start = (f32[128,128,32]{1,2,0:T(8,128)S(1)}, f32[128,128,32]{1,2,0:T(8,128)}, u32[]{:S(2)}) copy-start(f32[128,128,32]{1,2,0:T(8,128)} %fusion.166) | copy-start | bytes 6291460
  226.8 11.8 %copy-start.1 = (f32[128,128,32]{1,2,0:T(8,128)S(1)}, f32[128,128,32]{1,2,0:T(8,128)}, u32[]{:S(2)}) copy-start(f32[128,128,32]{1,2,0:T(8,128)} %fusion.148) | copy-start | bytes 6291460
  226.9 11.8 %copy-start.2 = (f32[128,128,32]{1,2,0:T(8,128)S(1)}, f32[128,128,32]{1,2,0:T(8,128)}, u32[]{:S(2)}) copy-start(f32[128,128,32]{1,2,0:T(8,128)} %fusion.168) | copy-start | bytes 6291460
  249.3 9.0 %copy-start.13 = (bf16[128,2048]{0,1:T(8,128)(2,1)S(1)}, bf16[128,2048]{0,1:T(8,128)(2,1)}, u32[]{:S(2)}) copy-start(bf16[128,2048]{0,1:T(8,128)(2,1)} %get-tuple-element.29) | copy-start | bytes 1572868
  250.2 20.0 %all-to-all-start.4 = ((bf16[128,16,128]{0,2,1:T(8,128)(2,1)}), bf16[128,16,128]{0,2,1:T(8,128)(2,1)S(1)}, u32[]{:S(2)}, u32[]{:S(2)}) async-start(bf16[128,16,128]{0,2,1:T(8,128)(2,1)} %bitcast.34), calls=%async_computation.4 | async-start | bytes 1048576 | tf_op jit(solution)/shard_map/all_to_all | solution.py:130
  260.6 10.1 %copy-start.10 = (bf16[128,2048]{0,1:T(8,128)(2,1)S(1)}, bf16[128,2048]{0,1:T(8,128)(2,1)}, u32[]{:S(2)}) copy-start(bf16[128,2048]{0,1:T(8,128)(2,1)} %copy-done.9) | copy-start | bytes 1572868
  260.6 10.1 %copy-start.12 = (bf16[128,2048]{0,1:T(8,128)(2,1)S(1)}, bf16[128,2048]{0,1:T(8,128)(2,1)}, u32[]{:S(2)}) copy-start(bf16[128,2048]{0,1:T(8,128)(2,1)} %copy-done.11) | copy-start | bytes 1572868
where the time goes:
time: 279 us; the launch traced here: 273 us
  matrix products  141 us (51%)
  waiting for transfers between devices  42.4 us (15%)
  local copies, waits for them, and re-layouts  29 us (10%)
  starting transfers between devices  26.7 us (10%)
  blocking collectives  23.1 us (8%)
  other arithmetic  9.14 us (3%)
    dot_general x24, matrix products, right_apply(): return jnp.einsum('cka,ab->ckb', blocks, table, precision=precise)  71.7 us
    dot_general x12, matrix products, left_apply(): return jnp.einsum('ka,cab->ckb', table, blocks, precision=precise)  69.6 us
    all_to_all x1, blocking collectives, per_device(): lax.all_to_all(gconv.T, 'ctx', split_axis=0, concat_axis=1, tiled=True)  19.4 us
    unnamed x42, local copies, waits for them, and re-layouts  13.3 us
    all_to_all x1, waiting for transfers between devices, per_device(): lax.all_to_all(mixed_rows.T, 'ctx', split_axis=0, concat_axis=1, tiled=True)  13 us
    all_to_all x1, waiting for transfers between devices, per_device(): lax.all_to_all(conv_cols, 'ctx', split_axis=1, concat_axis=0, tiled=True)  11 us
    all_to_all x1, waiting for transfers between devices, per_device(): lax.all_to_all(dmixed_cols, 'ctx', split_axis=1, concat_axis=0, tiled=True)  9.65 us
    all_to_all x1, waiting for transfers between devices, per_device(): lax.all_to_all(filter_taps.T, 'ctx', split_axis=0, concat_axis=1, tiled=T...  8.81 us
  transfers between devices with their start and end apart: 5, of which 4 were waited for; matrix products, arithmetic and copies ran while one was open for 14% of the time, Pallas kernels for 0%

commit v1 on v0

--- a/solution.py
+++ b/solution.py
@@ -2,7 +2,10 @@
 
 import jax
 import jax.numpy as jnp
+import numpy as np
 from jax import lax
+from jax.experimental import pallas as pl
+from jax.experimental.pallas import tpu as pltpu
 from jax.sharding import PartitionSpec as P
 
 precise = lax.Precision.HIGHEST
@@ -93,7 +96,7 @@
     return lax.psum(values, "tp")
 
 
-def per_device(query, key_proj, value_proj, filter_taps, grad_out):
+def per_device_plain(query, key_proj, value_proj, filter_taps, grad_out):
     length = query.shape[0] * lax.axis_size("ctx")
     width = query.shape[1] * lax.axis_size("tp")
     filter_scale = 1.0 / math.sqrt(length)
@@ -137,6 +140,338 @@
     return (mixer_out, dquery, dkey, dvalue, dtaps)
 
 
+LANES = 128
+ROWS = 16
+
+
+def odd_tables(block):
+    order = np.concatenate([np.arange(0, block, 2), np.arange(1, block, 2)])
+    angle = np.pi * np.outer(2 * order + 1, np.arange(block)) / (2 * block)
+    forward = np.concatenate([np.cos(angle), -np.sin(angle)], axis=0)
+    high = forward.astype(jnp.bfloat16)
+    low = (forward - high.astype(np.float64)).astype(jnp.bfloat16)
+    return high, low
+
+
+def params(flops, moved):
+    return dict(
+        compiler_params=pltpu.CompilerParams(vmem_limit_bytes=24 * 2**20),
+        cost_estimate=pl.CostEstimate(flops=flops, bytes_accessed=moved, transcendentals=0),
+    )
+
+
+def whole(count):
+    return [pl.BlockSpec(memory_space=pltpu.VMEM)] * count
+
+
+def pack_kernel(key_ref, value_ref, taps_ref, out_ref):
+    tokens = key_ref.shape[0]
+    for piece in range(out_ref.shape[0]):
+        cols = slice(piece * LANES, (piece + 1) * LANES)
+        key = key_ref[:, cols].astype(jnp.float32)
+        value = value_ref[:, cols].astype(jnp.float32)
+        out_ref[piece, :tokens, :] = (key * value).astype(jnp.bfloat16)
+        out_ref[piece, tokens:, :] = taps_ref[:, cols]
+
+
+def pack(key_proj, value_proj, taps):
+    tokens, width = key_proj.shape
+    pieces = width // LANES
+    step = 4 if pieces % 4 == 0 else pieces
+    wide = pl.BlockSpec((tokens, step * LANES), lambda i: (0, i))
+    return pl.pallas_call(
+        pack_kernel,
+        grid=(pieces // step,),
+        in_specs=[wide] * 3,
+        out_specs=pl.BlockSpec((step, 2 * tokens, LANES), lambda i: (i, 0, 0)),
+        out_shape=jax.ShapeDtypeStruct((pieces, 2 * tokens, LANES), jnp.bfloat16),
+        name="pack",
+        **params(tokens * width, 10 * tokens * width),
+    )(key_proj, value_proj, taps)
+
+
+def block_columns(ref, offset, tokens, block):
+    per = block // tokens
+    blocks = []
+    for b in range(ref.shape[0] // per):
+        parts = [ref[b * per + p, offset : offset + tokens, :] for p in range(per)]
+        blocks.append(jnp.concatenate(parts, axis=0))
+    return jnp.concatenate(blocks, axis=1)
+
+
+def to_spectrum(high_ref, low_ref, columns):
+    return jnp.dot(high_ref[...], columns, preferred_element_type=jnp.float32) + jnp.dot(
+        low_ref[...], columns, preferred_element_type=jnp.float32
+    )
+
+
+def store_signal(high_ref, low_ref, spec_ref, out_ref, offset, tokens, scale):
+    block = high_ref.shape[0]
+    per = block // tokens
+    spec = spec_ref[...]
+    signal = jnp.dot(high_ref[...], spec, preferred_element_type=jnp.float32) + jnp.dot(
+        low_ref[...], spec, preferred_element_type=jnp.float32
+    )
+    rounded = (signal * scale).astype(jnp.bfloat16)
+    for b in range(out_ref.shape[0] // per):
+        for p in range(per):
+            out_ref[b * per + p, offset : offset + tokens, :] = rounded[
+                p * tokens : (p + 1) * tokens, b * LANES : (b + 1) * LANES
+            ]
+
+
+def each_tile(block, body):
+    half = block // 2
+    for sign, base in ((1.0, 0), (-1.0, half)):
+
+        def step(i, carry, sign=sign, base=base):
+            body(pl.multiple_of(base + i * ROWS, ROWS), sign)
+            return carry
+
+        lax.fori_loop(0, half // ROWS, step, 0)
+
+
+def tile_of(ref, row, b, block):
+    cols = slice(b * LANES, (b + 1) * LANES)
+    return (ref[pl.ds(row, ROWS), cols], ref[pl.ds(row + block, ROWS), cols])
+
+
+def put_tile(ref, row, b, block, real, imag):
+    cols = slice(b * LANES, (b + 1) * LANES)
+    ref[pl.ds(row, ROWS), cols] = real.astype(ref.dtype)
+    ref[pl.ds(row + block, ROWS), cols] = imag.astype(ref.dtype)
+
+
+def forward_kernel(scale, in_ref, fh_ref, fl_ref, bh_ref, bl_ref, out_ref, mix_ref, tap_ref, acc_ref):
+    block = fh_ref.shape[1]
+    tokens = out_ref.shape[1]
+    count = mix_ref.shape[1] // LANES
+    mix_ref[...] = to_spectrum(fh_ref, fl_ref, block_columns(in_ref, 0, tokens, block))
+    tap_ref[...] = to_spectrum(fh_ref, fl_ref, block_columns(in_ref, tokens, tokens, block))
+
+    def body(row, sign):
+        taps = [tile_of(tap_ref, row, b, block) for b in range(count)]
+        before = None
+        for d in range(count):
+            real = imag = None
+            for j in range(d + 1):
+                mr, mi = tile_of(mix_ref, row, j, block)
+                tr, ti = taps[d - j]
+                re = mr * tr - mi * ti
+                im = mr * ti + mi * tr
+                real = re if real is None else real + re
+                imag = im if imag is None else imag + im
+            if before is None:
+                put_tile(acc_ref, row, d, block, real, imag)
+            elif sign > 0:
+                put_tile(acc_ref, row, d, block, real - before[1], imag + before[0])
+            else:
+                put_tile(acc_ref, row, d, block, real + before[1], imag - before[0])
+            before = (real, imag)
+
+    each_tile(block, body)
+    store_signal(bh_ref, bl_ref, acc_ref, out_ref, 0, tokens, scale)
+
+
+def backward_kernel(
+    scale, in_ref, mix_ref, tap_ref, fh_ref, fl_ref, bh_ref, bl_ref, out_ref, grad_ref, acc_ref
+):
+    block = fh_ref.shape[1]
+    tokens = in_ref.shape[1]
+    count = mix_ref.shape[1] // LANES
+    grad_ref[...] = to_spectrum(fh_ref, fl_ref, block_columns(in_ref, 0, tokens, block))
+    for which, other_ref in enumerate((tap_ref, mix_ref)):
+
+        def body(row, sign, other_ref=other_ref):
+            others = [tile_of(other_ref, row, b, block) for b in range(count)]
+            after = None
+            for d in reversed(range(count)):
+                real = imag = None
+                for k in range(count - d):
+                    gr, gi = tile_of(grad_ref, row, d + k, block)
+                    ar, ai = others[k]
+                    re = gr * ar + gi * ai
+                    im = gi * ar - gr * ai
+                    real = re if real is None else real + re
+                    imag = im if imag is None else imag + im
+                if after is None:
+                    put_tile(acc_ref, row, d, block, real, imag)
+                elif sign > 0:
+                    put_tile(acc_ref, row, d, block, real + after[1], imag - after[0])
+                else:
+                    put_tile(acc_ref, row, d, block, real - after[1], imag + after[0])
+                after = (real, imag)
+
+        each_tile(block, body)
+        store_signal(bh_ref, bl_ref, acc_ref, out_ref, which * tokens, tokens, scale)
+
+
+def convolve(received, tables, scale):
+    pieces, rows, _ = received.shape
+    tokens = rows // 2
+    fh, fl, bh, bl = tables
+    freq, block = fh.shape
+    wide = pieces * tokens // block * LANES
+    spectrum_shape = jax.ShapeDtypeStruct((freq, wide), jnp.float32)
+
+    def kernel(*refs):
+        forward_kernel(scale, *refs)
+
+    return pl.pallas_call(
+        kernel,
+        in_specs=whole(5),
+        out_specs=whole(3),
+        out_shape=(
+            jax.ShapeDtypeStruct((pieces, tokens, LANES), jnp.bfloat16),
+            spectrum_shape,
+            spectrum_shape,
+        ),
+        scratch_shapes=[pltpu.VMEM((freq, wide), jnp.bfloat16)],
+        name="forward",
+        **params(12 * freq * block * wide, 8 * freq * wide),
+    )(received, fh, fl, bh, bl)
+
+
+def correlate(received, mix, tap, tables, scale):
+    pieces, tokens, _ = received.shape
+    fh, fl, bh, bl = tables
+    freq, block = fh.shape
+    wide = mix.shape[1]
+
+    def kernel(*refs):
+        backward_kernel(scale, *refs)
+
+    return pl.pallas_call(
+        kernel,
+        in_specs=whole(7),
+        out_specs=pl.BlockSpec(memory_space=pltpu.VMEM),
+        out_shape=jax.ShapeDtypeStruct((pieces, 2 * tokens, LANES), jnp.bfloat16),
+        scratch_shapes=[
+            pltpu.VMEM((freq, wide), jnp.float32),
+            pltpu.VMEM((freq, wide), jnp.bfloat16),
+        ],
+        name="backward",
+        **params(12 * freq * block * wide, 8 * freq * wide),
+    )(received, mix, tap, fh, fl, bh, bl)
+
+
+def sums_kernel(query_ref, up_ref, conv_ref, out_ref):
+    tokens = query_ref.shape[0]
+    square = jnp.zeros((tokens, LANES), jnp.float32)
+    cross = jnp.zeros((tokens, LANES), jnp.float32)
+    for piece in range(conv_ref.shape[0]):
+        cols = slice(piece * LANES, (piece + 1) * LANES)
+        gated = query_ref[:, cols].astype(jnp.float32) * conv_ref[piece].astype(jnp.float32)
+        square += gated * gated
+        cross += up_ref[:, cols].astype(jnp.float32) * gated
+    out_ref[0:1, :] = jnp.sum(square.T, axis=0, keepdims=True)
+    out_ref[1:2, :] = jnp.sum(cross.T, axis=0, keepdims=True)
+
+
+def token_sums(query, upstream, conv):
+    tokens, width = query.shape
+    return pl.pallas_call(
+        sums_kernel,
+        in_specs=whole(3),
+        out_specs=pl.BlockSpec(memory_space=pltpu.VMEM),
+        out_shape=jax.ShapeDtypeStruct((2, tokens), jnp.float32),
+        name="sums",
+        **params(5 * tokens * width, 6 * tokens * width),
+    )(query, upstream, conv)
+
+
+def norm_kernel(channels, sums_ref, query_ref, up_ref, conv_ref, mixer_ref, dquery_ref, grad_ref):
+    tokens = query_ref.shape[0]
+    mean = sums_ref[0:1, :] / channels
+    dots = sums_ref[1:2, :] / channels
+    inverse_row = lax.rsqrt(mean + 1e-05)
+    slope_row = inverse_row * inverse_row * inverse_row * dots
+    inverse = jnp.broadcast_to(inverse_row, (LANES, tokens)).T
+    slope = jnp.broadcast_to(slope_row, (LANES, tokens)).T
+    for piece in range(conv_ref.shape[0]):
+        cols = slice(piece * LANES, (piece + 1) * LANES)
+        conv = conv_ref[piece].astype(jnp.float32)
+        query = query_ref[:, cols].astype(jnp.float32)
+        gated = query * conv
+        mixer_ref[:, cols] = (gated * inverse).astype(jnp.bfloat16)
+        dgated = inverse * up_ref[:, cols].astype(jnp.float32) - slope * gated
+        dquery_ref[:, cols] = (dgated * conv).astype(jnp.bfloat16)
+        grad_ref[piece] = (dgated * query).astype(jnp.bfloat16)
+
+
+def gate_norm(sums, query, upstream, conv, channels):
+    tokens, width = query.shape
+
+    def kernel(*refs):
+        norm_kernel(channels, *refs)
+
+    flat = jax.ShapeDtypeStruct((tokens, width), jnp.bfloat16)
+    return pl.pallas_call(
+        kernel,
+        in_specs=whole(4),
+        out_specs=whole(3),
+        out_shape=(flat, flat, jax.ShapeDtypeStruct(conv.shape, jnp.bfloat16)),
+        name="norm",
+        **params(8 * tokens * width, 12 * tokens * width),
+    )(sums, query, upstream, conv)
+
+
+def unpack_kernel(back_ref, key_ref, value_ref, dkey_ref, dvalue_ref, dtaps_ref):
+    tokens = key_ref.shape[0]
+    for piece in range(back_ref.shape[0]):
+        cols = slice(piece * LANES, (piece + 1) * LANES)
+        dmixed = back_ref[piece, :tokens, :].astype(jnp.float32)
+        dkey_ref[:, cols] = (dmixed * value_ref[:, cols].astype(jnp.float32)).astype(jnp.bfloat16)
+        dvalue_ref[:, cols] = (dmixed * key_ref[:, cols].astype(jnp.float32)).astype(jnp.bfloat16)
+        dtaps_ref[:, cols] = back_ref[piece, tokens:, :]
+
+
+def unpack(back, key_proj, value_proj):
+    tokens, width = key_proj.shape
+    pieces = width // LANES
+    step = 4 if pieces % 4 == 0 else pieces
+    wide = pl.BlockSpec((tokens, step * LANES), lambda i: (0, i))
+    flat = jax.ShapeDtypeStruct((tokens, width), jnp.bfloat16)
+    return pl.pallas_call(
+        unpack_kernel,
+        grid=(pieces // step,),
+        in_specs=[pl.BlockSpec((step, 2 * tokens, LANES), lambda i: (i, 0, 0)), wide, wide],
+        out_specs=[wide] * 3,
+        out_shape=(flat, flat, flat),
+        name="unpack",
+        **params(2 * tokens * width, 14 * tokens * width),
+    )(back, key_proj, value_proj)
+
+
+def exchange(pieces):
+    return lax.all_to_all(pieces, "ctx", split_axis=0, concat_axis=0, tiled=True)
+
+
+def per_device_kernels(query, key_proj, value_proj, filter_taps, grad_out):
+    length = query.shape[0] * lax.axis_size("ctx")
+    width = query.shape[1] * lax.axis_size("tp")
+    block = 2 * query.shape[0]
+    scale = 1.0 / (math.sqrt(length) * block)
+    high, low = odd_tables(block)
+    tables = tuple(jnp.asarray(t) for t in (high, low, high.T.copy(), low.T.copy()))
+    received = exchange(pack(key_proj, value_proj, filter_taps))
+    conv_cols, mix, tap = convolve(received, tables, scale)
+    conv = exchange(conv_cols)
+    sums = channel_total(token_sums(query, grad_out, conv))
+    mixer_out, dquery, grad_rows = gate_norm(sums, query, grad_out, conv, width)
+    back_cols = correlate(exchange(grad_rows), mix, tap, tables, scale)
+    dkey, dvalue, dtaps = unpack(exchange(back_cols), key_proj, value_proj)
+    return (mixer_out, dquery, dkey, dvalue, dtaps)
+
+
+def per_device(query, key_proj, value_proj, filter_taps, grad_out):
+    tokens, width = query.shape
+    ring = lax.axis_size("ctx")
+    if width == ring * LANES and tokens == LANES and ring % 2 == 0:
+        return per_device_kernels(query, key_proj, value_proj, filter_taps, grad_out)
+    return per_device_plain(query, key_proj, value_proj, filter_taps, grad_out)
+
+
 def solution(mesh):
     in_specs = (P("ctx", "tp"), P("ctx", "tp"), P("ctx", "tp"), P("ctx", "tp"), P("ctx", "tp"))
     out_specs = (P("ctx", "tp"), P("ctx", "tp"), P("ctx", "tp"), P("ctx", "tp"), P("ctx", "tp"))

time: 279 us -> 124 us (0.44); the launches traced: 273 us -> 123 us
  matrix products: 141 us -> 0 us
  blocking collectives: 23.1 us -> 103 us
  waiting for transfers between devices: 42.4 us -> 0 us
  starting transfers between devices: 26.7 us -> 0 us
  local copies, waits for them, and re-layouts: 29 us -> 6.49 us
  Pallas kernels: 0 us -> 12.9 us
  other arithmetic: 9.14 us -> 0 us
    dot_general x36 -> x0, matrix products: 141 us -> none  [the longest x24 71.7 us: right_apply(): return jnp.einsum('cka,ab->ckb', blocks, table, precision=precise)]
    all_to_all x1 -> x4, blocking collectives: 19.4 us -> 99.6 us  [exchange(): lax.all_to_all(pieces, 'ctx', split_axis=0, concat_axis=0, tiled=True)]
    all_to_all x5 -> x0, waiting for transfers between devices: 42.4 us -> none  [the longest x1 13 us: per_device(): lax.all_to_all(mixed_rows.T, 'ctx', split_axis=0, concat_axis=1, tiled=True)]
    all_to_all x5 -> x0, starting transfers between devices: 26.7 us -> none  [the longest x1 7.31 us: per_device(): lax.all_to_all(mixed_rows.T, 'ctx', split_axis=0, concat_axis=1, tiled=True)]
    pallas_call x0 -> x6, Pallas kernels: none -> 12.9 us  [the longest x1 5.22 us: correlate(): pl.pallas_call(kernel, in_specs=whole(7), out_specs=pl.BlockSpec(memory_s...]
    convert_element_type x8 -> x0, other arithmetic: 7.53 us -> none  [the longest x1 2.58 us: per_device(): gconv = (dgated * query_float).astype(jnp.bfloat16)]
    unnamed x42 -> x34, local copies, waits for them, and re-layouts: 13.3 us -> 6.49 us
    reshape x3 -> x0, local copies, waits for them, and re-layouts: 5.73 us -> none  [spectrum(): padded = padded.reshape(channels, row_count, col_count)]
  transfers between devices with their start and end apart: 5 -> 0, of which waited for: 4 -> 0; matrix products, arithmetic and copies ran while one was open for 14% -> 0% of each run, Pallas kernels for 0% -> 0%
where the time goes in v1:
time: 124 us; the launch traced here: 123 us
  blocking collectives  103 us (83%)
  Pallas kernels  12.9 us (10%)
  local copies, waits for them, and re-layouts  6.49 us (5%)
    all_to_all x4, blocking collectives, exchange(): lax.all_to_all(pieces, 'ctx', split_axis=0, concat_axis=0, tiled=True)  99.6 us
    unnamed x34, local copies, waits for them, and re-layouts  6.49 us
    pallas_call x1, Pallas kernels, correlate(): pl.pallas_call(kernel, in_specs=whole(7), out_specs=pl.BlockSpec(memory_s...  5.22 us
    psum x1, blocking collectives, channel_total(): return lax.psum(values, 'tp')  3.78 us
    pallas_call x1, Pallas kernels, convolve(): pl.pallas_call(kernel, in_specs=whole(5), out_specs=whole(3), out_shape=(...  3.52 us

profile of v1, /device:TPU:1, one launch (start us, length us, event | category | flops | bytes accessed | tf_op | source)
XLA Modules:
  0.0 123.5 jit_solution(18140870391254134620)
XLA Ops:
  0.6 0.0 copy-start.2
  0.6 1.0 copy-done.2
  1.7 1.0 copy-done.4
  2.7 1.0 copy-done.9
  3.8 0.4 pack.1
  4.2 32.3 %all_to_all.20.refs_0_ = bf16[16,256,128]{2,1,0:T(8,128)(2,1)S(1)} all-to-all(bf16[16,256,128]{2,1,0:T(8,128)(2,1)S(1)} %pack.1), channel_id=1, replica_groups=mesh['ctx'=16,'tp'=2] {'ctx'}, dimensions={0} | all-to-all | bytes 2097152 | tf_op jit(solution)/shard_map/all_to_all | solution.py:447
  36.5 0.0 copy-start.6
  36.5 0.0 copy-start.7
  36.5 3.5 %forward.1 = (bf16[16,128,128]{2,1,0:T(8,128)(2,1)S(1)}, f32[512,1024]{1,0:T(8,128)S(1)}, f32[512,1024]{1,0:T(8,128)S(1)}) custom-call(bf16[16,256,128]{2,1,0:T(8,128)(2,1)S(1)} %all_to_all.20.refs_0_, bf16[512,256]{1,0:T(8,128)(2,1)S(1)} %copy-done.15, bf16[512,256]{1,0:T(8,128)(2,1)S(1)} %copy-done.13, bf16[256,512]{1,0:T(8,128)(2,1)S(1)} %copy-done.11, ...), custom_call_target="tpu_custom_call" | custom-call | flops 1610612736 | bytes 4194304 | tf_op jit(solution)/shard_map/forward/pallas_call | solution.py:320
  40.1 1.3 %copy-done = f32[512,1024]{1,0:T(8,128)} copy-done((f32[512,1024]{1,0:T(8,128)}, f32[512,1024]{1,0:T(8,128)S(1)}, u32[]{:S(2)}) %copy-start) | copy-done | bytes 2097176
  41.4 18.3 %all_to_all.21.conv_ref.refs_3_ = bf16[16,128,128]{2,1,0:T(8,128)(2,1)S(1)} all-to-all(bf16[16,128,128]{2,1,0:T(8,128)(2,1)S(1)} %get-tuple-element.14), channel_id=1, replica_groups=mesh['ctx'=16,'tp'=2] {'ctx'}, dimensions={0} | all-to-all | bytes 1048576 | tf_op jit(solution)/shard_map/all_to_all | solution.py:447
  59.7 0.0 copy-done.6
  59.7 0.4 sums.1
  60.0 3.8 %psum.7.refs_0_ = f32[2,128]{1,0:T(2,128)S(1)} all-reduce(f32[2,128]{1,0:T(2,128)S(1)} %sums.1), channel_id=1, replica_groups=mesh['ctx'=16,'tp'=2] {'tp'}, use_global_device_ids=true, to_apply=%region_0.0 | all-reduce | flops 256 | bytes 2048 | tf_op jit(solution)/shard_map/psum | solution.py:96
  63.8 1.0 copy-done.8
  64.9 1.6 %norm.1 = (bf16[128,2048]{1,0:T(8,128)(2,1)}, bf16[128,2048]{1,0:T(8,128)(2,1)}, bf16[16,128,128]{2,1,0:T(8,128)(2,1)S(1)}) custom-call(f32[2,128]{1,0:T(2,128)S(1)} %psum.7.refs_0_, bf16[128,2048]{1,0:T(8,128)(2,1)S(1)} %copy-done.6, bf16[128,2048]{1,0:T(8,128)(2,1)S(1)} %copy-done.8, bf16[16,128,128]{2,1,0:T(8,128)(2,1)S(1)} %all_to_all.21.conv_ref.refs_3_), custom_call_target="tpu_custom_call" | custom-call | flops 2097152 | bytes 3145728 | tf_op jit(solution)/shard_map/norm/pallas_call | solution.py:409
  66.5 19.4 %all_to_all.22.refs_0_ = bf16[16,128,128]{2,1,0:T(8,128)(2,1)S(1)} all-to-all(bf16[16,128,128]{2,1,0:T(8,128)(2,1)S(1)} %get-tuple-element.17), channel_id=1, replica_groups=mesh['ctx'=16,'tp'=2] {'ctx'}, dimensions={0} | all-to-all | bytes 1048576 | tf_op jit(solution)/shard_map/all_to_all | solution.py:447
  85.9 0.0 copy-start.16
  85.9 0.9 copy-done.16
  86.8 5.2 %backward.1 = bf16[16,256,128]{2,1,0:T(8,128)(2,1)S(1)} custom-call(bf16[16,128,128]{2,1,0:T(8,128)(2,1)S(1)} %all_to_all.22.refs_0_, f32[512,1024]{1,0:T(8,128)S(1)} %get-tuple-element.18.refs_1_, f32[512,1024]{1,0:T(8,128)S(1)} %copy-done.1, bf16[512,256]{1,0:T(8,128)(2,1)S(1)} %copy-done.16, bf16[512,256]{1,0:T(8,128)(2,1)S(1)} %copy-done.14, ...), custom_call_target="tpu_custom_call" | custom-call | flops 1610612736 | bytes 4194304 | tf_op jit(solution)/shard_map/backward/pallas_call | solution.py:344
  92.1 0.0 copy-start.3
  92.1 0.0 copy-start.5
  92.1 29.6 %all_to_all.23.back_ref = bf16[16,256,128]{2,1,0:T(8,128)(2,1)S(1)} all-to-all(bf16[16,256,128]{2,1,0:T(8,128)(2,1)S(1)} %backward.1), channel_id=1, replica_groups=mesh['ctx'=16,'tp'=2] {'ctx'}, dimensions={0} | all-to-all | bytes 2097152 | tf_op jit(solution)/shard_map/all_to_all | solution.py:447
  121.7 1.8 %unpack.1 = (bf16[128,2048]{1,0:T(8,128)(2,1)}, bf16[128,2048]{1,0:T(8,128)(2,1)}, bf16[128,2048]{1,0:T(8,128)(2,1)}) custom-call(bf16[16,256,128]{2,1,0:T(8,128)(2,1)S(1)} %all_to_all.23.back_ref, bf16[128,2048]{1,0:T(8,128)(2,1)S(1)} %copy-done.3, bf16[128,2048]{1,0:T(8,128)(2,1)S(1)} %copy-done.5), custom_call_target="tpu_custom_call" | custom-call | flops 524288 | bytes 3670016 | tf_op jit(solution)/shard_map/unpack/pallas_call | solution.py:435
  (21 shorter events, 0.0 us)
Async XLA Ops:
  0.6 1.0 copy-start.2
  1.7 1.0 copy-start.4
  2.7 1.0 copy-start.9
  3.8 32.7 %copy-start.10 = (bf16[256,512]{1,0:T(8,128)(2,1)S(1)}, bf16[256,512]{1,0:T(8,128)(2,1)}, u32[]{:S(2)}) copy-start(bf16[256,512]{1,0:T(8,128)(2,1)} %constant.11.clone.refs_4_.refs_6_) | copy-start | bytes 786436
  3.8 32.7 %copy-start.11 = (bf16[256,512]{1,0:T(8,128)(2,1)S(1)}, bf16[256,512]{1,0:T(8,128)(2,1)}, u32[]{:S(2)}) copy-start(bf16[256,512]{1,0:T(8,128)(2,1)} %constant.10.clone.refs_3_.refs_5_) | copy-start | bytes 786436
  3.8 32.7 %copy-start.13 = (bf16[512,256]{1,0:T(8,128)(2,1)S(1)}, bf16[512,256]{1,0:T(8,128)(2,1)}, u32[]{:S(2)}) copy-start(bf16[512,256]{1,0:T(8,128)(2,1)} %constant.9.clone.refs_2_.refs_4_) | copy-start | bytes 786436
  3.8 32.7 %copy-start.15 = (bf16[512,256]{1,0:T(8,128)(2,1)S(1)}, bf16[512,256]{1,0:T(8,128)(2,1)}, u32[]{:S(2)}) copy-start(bf16[512,256]{1,0:T(8,128)(2,1)} %constant.8.clone.refs_1_.refs_3_) | copy-start | bytes 786436
  36.5 23.2 %copy-start.6 = (bf16[128,2048]{1,0:T(8,128)(2,1)S(1)}, bf16[128,2048]{1,0:T(8,128)(2,1)}, u32[]{:S(2)}) copy-start(bf16[128,2048]{1,0:T(8,128)(2,1)} %refs_1_.2) | copy-start | bytes 1572868
  36.5 23.1 %copy-start.7 = (bf16[128,2048]{1,0:T(8,128)(2,1)S(1)}, bf16[128,2048]{1,0:T(8,128)(2,1)}, u32[]{:S(2)}) copy-start(bf16[128,2048]{1,0:T(8,128)(2,1)} %refs_2_.2) | copy-start | bytes 1572868
  40.1 1.3 %copy-start = (f32[512,1024]{1,0:T(8,128)}, f32[512,1024]{1,0:T(8,128)S(1)}, u32[]{:S(2)}) copy-start(f32[512,1024]{1,0:T(8,128)S(1)} %get-tuple-element.19.refs_2_) | copy-start | bytes 6291460
  63.8 1.0 copy-start.8
  64.9 21.0 %copy-start.1 = (f32[512,1024]{1,0:T(8,128)S(1)}, f32[512,1024]{1,0:T(8,128)}, u32[]{:S(2)}) copy-start(f32[512,1024]{1,0:T(8,128)} %copy-done) | copy-start | bytes 6291460
  64.9 21.0 %copy-start.12 = (bf16[256,512]{1,0:T(8,128)(2,1)S(1)}, bf16[256,512]{1,0:T(8,128)(2,1)}, u32[]{:S(2)}) copy-start(bf16[256,512]{1,0:T(8,128)(2,1)} %constant.10.clone.refs_3_.refs_5_) | copy-start | bytes 786436
  64.9 21.0 %copy-start.14 = (bf16[512,256]{1,0:T(8,128)(2,1)S(1)}, bf16[512,256]{1,0:T(8,128)(2,1)}, u32[]{:S(2)}) copy-start(bf16[512,256]{1,0:T(8,128)(2,1)} %constant.9.clone.refs_2_.refs_4_) | copy-start | bytes 786436
  85.9 1.0 copy-start.16
  92.1 29.6 %copy-start.3 = (bf16[128,2048]{1,0:T(8,128)(2,1)S(1)}, bf16[128,2048]{1,0:T(8,128)(2,1)}, u32[]{:S(2)}) copy-start(bf16[128,2048]{1,0:T(8,128)(2,1)} %key_ref.3) | copy-start | bytes 1572868
  92.1 29.6 %copy-start.5 = (bf16[128,2048]{1,0:T(8,128)(2,1)S(1)}, bf16[128,2048]{1,0:T(8,128)(2,1)}, u32[]{:S(2)}) copy-start(bf16[128,2048]{1,0:T(8,128)(2,1)} %value_ref.3) | copy-start | bytes 1572868

commit v2 on v1

--- a/solution.py
+++ b/solution.py
@@ -142,20 +142,19 @@
 
 LANES = 128
 ROWS = 16
+STEPS = 4
 
 
 def odd_tables(block):
     order = np.concatenate([np.arange(0, block, 2), np.arange(1, block, 2)])
     angle = np.pi * np.outer(2 * order + 1, np.arange(block)) / (2 * block)
-    forward = np.concatenate([np.cos(angle), -np.sin(angle)], axis=0)
-    high = forward.astype(jnp.bfloat16)
-    low = (forward - high.astype(np.float64)).astype(jnp.bfloat16)
-    return high, low
-
-
-def params(flops, moved):
+    forward = np.concatenate([np.cos(angle), -np.sin(angle)], axis=0).astype(jnp.bfloat16)
+    return jnp.asarray(forward), jnp.asarray(forward.T.copy())
+
+
+def params(flops, moved, limit=16):
     return dict(
-        compiler_params=pltpu.CompilerParams(vmem_limit_bytes=24 * 2**20),
+        compiler_params=pltpu.CompilerParams(vmem_limit_bytes=limit * 2**20),
         cost_estimate=pl.CostEstimate(flops=flops, bytes_accessed=moved, transcendentals=0),
     )
 
@@ -164,30 +163,64 @@
     return [pl.BlockSpec(memory_space=pltpu.VMEM)] * count
 
 
-def pack_kernel(key_ref, value_ref, taps_ref, out_ref):
-    tokens = key_ref.shape[0]
-    for piece in range(out_ref.shape[0]):
-        cols = slice(piece * LANES, (piece + 1) * LANES)
-        key = key_ref[:, cols].astype(jnp.float32)
-        value = value_ref[:, cols].astype(jnp.float32)
-        out_ref[piece, :tokens, :] = (key * value).astype(jnp.bfloat16)
-        out_ref[piece, tokens:, :] = taps_ref[:, cols]
+def started(copies):
+    for copy in copies:
+        copy.start()
+    return copies
+
+
+def pack_kernel(
+    key_hbm, value_hbm, taps_hbm, out_hbm, key_ref, value_ref, stage_ref, in_sems, tap_sems, out_sems
+):
+    pieces = stage_ref.shape[0]
+    share = pieces // STEPS
+    loads = []
+    for i in range(STEPS):
+        wide = slice(i * share * LANES, (i + 1) * share * LANES)
+        group = [
+            pltpu.make_async_copy(key_hbm.at[:, wide], key_ref.at[:, wide], in_sems.at[0, i]),
+            pltpu.make_async_copy(value_hbm.at[:, wide], value_ref.at[:, wide], in_sems.at[1, i]),
+        ]
+        for piece in range(i * share, (i + 1) * share):
+            col = slice(piece * LANES, (piece + 1) * LANES)
+            group.append(
+                pltpu.make_async_copy(taps_hbm.at[:, col], stage_ref.at[piece, 1], tap_sems.at[piece])
+            )
+        loads.append(started(group))
+    stores = []
+    for i, group in enumerate(loads):
+        for copy in group:
+            copy.wait()
+        for piece in range(i * share, (i + 1) * share):
+            col = slice(piece * LANES, (piece + 1) * LANES)
+            product = key_ref[:, col].astype(jnp.float32) * value_ref[:, col].astype(jnp.float32)
+            stage_ref[piece, 0] = product.astype(jnp.bfloat16)
+        part = pl.ds(i * share, share)
+        stores += started([pltpu.make_async_copy(stage_ref.at[part], out_hbm.at[part], out_sems.at[i])])
+    for copy in stores:
+        copy.wait()
 
 
 def pack(key_proj, value_proj, taps):
     tokens, width = key_proj.shape
     pieces = width // LANES
-    step = 4 if pieces % 4 == 0 else pieces
-    wide = pl.BlockSpec((tokens, step * LANES), lambda i: (0, i))
-    return pl.pallas_call(
+    packed = pl.pallas_call(
         pack_kernel,
-        grid=(pieces // step,),
-        in_specs=[wide] * 3,
-        out_specs=pl.BlockSpec((step, 2 * tokens, LANES), lambda i: (i, 0, 0)),
-        out_shape=jax.ShapeDtypeStruct((pieces, 2 * tokens, LANES), jnp.bfloat16),
+        in_specs=[pl.BlockSpec(memory_space=pltpu.HBM)] * 3,
+        out_specs=pl.BlockSpec(memory_space=pltpu.HBM),
+        out_shape=jax.ShapeDtypeStruct((pieces, 2, tokens, LANES), jnp.bfloat16),
+        scratch_shapes=[
+            pltpu.VMEM((tokens, width), jnp.bfloat16),
+            pltpu.VMEM((tokens, width), jnp.bfloat16),
+            pltpu.VMEM((pieces, 2, tokens, LANES), jnp.bfloat16),
+            pltpu.SemaphoreType.DMA((2, STEPS)),
+            pltpu.SemaphoreType.DMA((pieces,)),
+            pltpu.SemaphoreType.DMA((STEPS,)),
+        ],
         name="pack",
-        **params(tokens * width, 10 * tokens * width),
+        **params(tokens * width, 10 * tokens * width, 63),
     )(key_proj, value_proj, taps)
+    return packed.reshape(pieces, 2 * tokens, LANES)
 
 
 def block_columns(ref, offset, tokens, block):
@@ -199,19 +232,13 @@
     return jnp.concatenate(blocks, axis=1)
 
 
-def to_spectrum(high_ref, low_ref, columns):
-    return jnp.dot(high_ref[...], columns, preferred_element_type=jnp.float32) + jnp.dot(
-        low_ref[...], columns, preferred_element_type=jnp.float32
-    )
-
-
-def store_signal(high_ref, low_ref, spec_ref, out_ref, offset, tokens, scale):
-    block = high_ref.shape[0]
-    per = block // tokens
-    spec = spec_ref[...]
-    signal = jnp.dot(high_ref[...], spec, preferred_element_type=jnp.float32) + jnp.dot(
-        low_ref[...], spec, preferred_element_type=jnp.float32
-    )
+def to_spectrum(table_ref, columns):
+    return jnp.dot(table_ref[...], columns, preferred_element_type=jnp.float32)
+
+
+def store_signal(back_ref, spec_ref, out_ref, offset, tokens, scale):
+    per = back_ref.shape[0] // tokens
+    signal = jnp.dot(back_ref[...], spec_ref[...], preferred_element_type=jnp.float32)
     rounded = (signal * scale).astype(jnp.bfloat16)
     for b in range(out_ref.shape[0] // per):
         for p in range(per):
@@ -242,25 +269,29 @@
     ref[pl.ds(row + block, ROWS), cols] = imag.astype(ref.dtype)
 
 
-def forward_kernel(scale, in_ref, fh_ref, fl_ref, bh_ref, bl_ref, out_ref, mix_ref, tap_ref, acc_ref):
-    block = fh_ref.shape[1]
-    tokens = out_ref.shape[1]
+def plus(total, term):
+    return term if total is None else total + term
+
+
+def forward_products(mix_ref, tap_ref, acc_ref, block):
     count = mix_ref.shape[1] // LANES
-    mix_ref[...] = to_spectrum(fh_ref, fl_ref, block_columns(in_ref, 0, tokens, block))
-    tap_ref[...] = to_spectrum(fh_ref, fl_ref, block_columns(in_ref, tokens, tokens, block))
 
     def body(row, sign):
         taps = [tile_of(tap_ref, row, b, block) for b in range(count)]
+        taps = [(r, i, r + i) for r, i in taps]
+        mixes = [tile_of(mix_ref, row, b, block) for b in range(count)]
+        mixes = [(r, i, r + i) for r, i in mixes]
         before = None
         for d in range(count):
-            real = imag = None
+            first = second = third = None
             for j in range(d + 1):
-                mr, mi = tile_of(mix_ref, row, j, block)
-                tr, ti = taps[d - j]
-                re = mr * tr - mi * ti
-                im = mr * ti + mi * tr
-                real = re if real is None else real + re
-                imag = im if imag is None else imag + im
+                mr, mi, ms = mixes[j]
+                tr, ti, ts = taps[d - j]
+                first = plus(first, mr * tr)
+                second = plus(second, mi * ti)
+                third = plus(third, ms * ts)
+            real = first - second
+            imag = third - first - second
             if before is None:
                 put_tile(acc_ref, row, d, block, real, imag)
             elif sign > 0:
@@ -270,89 +301,105 @@
             before = (real, imag)
 
     each_tile(block, body)
-    store_signal(bh_ref, bl_ref, acc_ref, out_ref, 0, tokens, scale)
+
+
+def backward_products(grad_ref, other_ref, acc_ref, block):
+    count = grad_ref.shape[1] // LANES
+
+    def body(row, sign):
+        others = [tile_of(other_ref, row, b, block) for b in range(count)]
+        others = [(r, i, r - i) for r, i in others]
+        grads = [tile_of(grad_ref, row, b, block) for b in range(count)]
+        grads = [(r, i, r + i) for r, i in grads]
+        after = None
+        for d in reversed(range(count)):
+            first = second = third = None
+            for k in range(count - d):
+                gr, gi, gs = grads[d + k]
+                ar, ai, ad = others[k]
+                first = plus(first, gr * ar)
+                second = plus(second, gi * ai)
+                third = plus(third, gs * ad)
+            real = first + second
+            imag = third - first + second
+            if after is None:
+                put_tile(acc_ref, row, d, block, real, imag)
+            elif sign > 0:
+                put_tile(acc_ref, row, d, block, real + after[1], imag - after[0])
+            else:
+                put_tile(acc_ref, row, d, block, real - after[1], imag + after[0])
+            after = (real, imag)
+
+    each_tile(block, body)
+
+
+def forward_kernel(scale, in_ref, table_ref, back_ref, out_ref, mix_ref, tap_ref, acc_ref):
+    block = table_ref.shape[1]
+    tokens = out_ref.shape[1]
+    mix_ref[...] = to_spectrum(table_ref, block_columns(in_ref, 0, tokens, block))
+    tap_ref[...] = to_spectrum(table_ref, block_columns(in_ref, tokens, tokens, block))
+    forward_products(mix_ref, tap_ref, acc_ref, block)
+    store_signal(back_ref, acc_ref, out_ref, 0, tokens, scale)
 
 
 def backward_kernel(
-    scale, in_ref, mix_ref, tap_ref, fh_ref, fl_ref, bh_ref, bl_ref, out_ref, grad_ref, acc_ref
+    scale, grad_in_ref, in_ref, table_ref, back_ref, out_ref, grad_ref, other_ref, acc_ref
 ):
-    block = fh_ref.shape[1]
-    tokens = in_ref.shape[1]
-    count = mix_ref.shape[1] // LANES
-    grad_ref[...] = to_spectrum(fh_ref, fl_ref, block_columns(in_ref, 0, tokens, block))
-    for which, other_ref in enumerate((tap_ref, mix_ref)):
-
-        def body(row, sign, other_ref=other_ref):
-            others = [tile_of(other_ref, row, b, block) for b in range(count)]
-            after = None
-            for d in reversed(range(count)):
-                real = imag = None
-                for k in range(count - d):
-                    gr, gi = tile_of(grad_ref, row, d + k, block)
-                    ar, ai = others[k]
-                    re = gr * ar + gi * ai
-                    im = gi * ar - gr * ai
-                    real = re if real is None else real + re
-                    imag = im if imag is None else imag + im
-                if after is None:
-                    put_tile(acc_ref, row, d, block, real, imag)
-                elif sign > 0:
-                    put_tile(acc_ref, row, d, block, real + after[1], imag - after[0])
-                else:
-                    put_tile(acc_ref, row, d, block, real - after[1], imag + after[0])
-                after = (real, imag)
-
-        each_tile(block, body)
-        store_signal(bh_ref, bl_ref, acc_ref, out_ref, which * tokens, tokens, scale)
+    block = table_ref.shape[1]
+    tokens = grad_in_ref.shape[1]
+    grad_ref[...] = to_spectrum(table_ref, block_columns(grad_in_ref, 0, tokens, block))
+    for which in range(2):
+        columns = block_columns(in_ref, (1 - which) * tokens, tokens, block)
+        other_ref[...] = to_spectrum(table_ref, columns)
+        backward_products(grad_ref, other_ref, acc_ref, block)
+        store_signal(back_ref, acc_ref, out_ref, which * tokens, tokens, scale)
 
 
 def convolve(received, tables, scale):
     pieces, rows, _ = received.shape
     tokens = rows // 2
-    fh, fl, bh, bl = tables
-    freq, block = fh.shape
+    freq, block = tables[0].shape
     wide = pieces * tokens // block * LANES
-    spectrum_shape = jax.ShapeDtypeStruct((freq, wide), jnp.float32)
 
     def kernel(*refs):
         forward_kernel(scale, *refs)
 
     return pl.pallas_call(
         kernel,
-        in_specs=whole(5),
-        out_specs=whole(3),
-        out_shape=(
-            jax.ShapeDtypeStruct((pieces, tokens, LANES), jnp.bfloat16),
-            spectrum_shape,
-            spectrum_shape,
-        ),
-        scratch_shapes=[pltpu.VMEM((freq, wide), jnp.bfloat16)],
+        in_specs=whole(3),
+        out_specs=pl.BlockSpec(memory_space=pltpu.VMEM),
+        out_shape=jax.ShapeDtypeStruct((pieces, tokens, LANES), jnp.bfloat16),
+        scratch_shapes=[
+            pltpu.VMEM((freq, wide), jnp.float32),
+            pltpu.VMEM((freq, wide), jnp.float32),
+            pltpu.VMEM((freq, wide), jnp.bfloat16),
+        ],
         name="forward",
-        **params(12 * freq * block * wide, 8 * freq * wide),
-    )(received, fh, fl, bh, bl)
-
-
-def correlate(received, mix, tap, tables, scale):
-    pieces, tokens, _ = received.shape
-    fh, fl, bh, bl = tables
-    freq, block = fh.shape
-    wide = mix.shape[1]
+        **params(6 * freq * block * wide, 8 * freq * wide),
+    )(received, *tables)
+
+
+def correlate(grads, received, tables, scale):
+    pieces, tokens, _ = grads.shape
+    freq, block = tables[0].shape
+    wide = pieces * tokens // block * LANES
 
     def kernel(*refs):
         backward_kernel(scale, *refs)
 
     return pl.pallas_call(
         kernel,
-        in_specs=whole(7),
+        in_specs=whole(4),
         out_specs=pl.BlockSpec(memory_space=pltpu.VMEM),
         out_shape=jax.ShapeDtypeStruct((pieces, 2 * tokens, LANES), jnp.bfloat16),
         scratch_shapes=[
             pltpu.VMEM((freq, wide), jnp.float32),
+            pltpu.VMEM((freq, wide), jnp.float32),
             pltpu.VMEM((freq, wide), jnp.bfloat16),
         ],
         name="backward",
-        **params(12 * freq * block * wide, 8 * freq * wide),
-    )(received, mix, tap, fh, fl, bh, bl)
+        **params(10 * freq * block * wide, 8 * freq * wide),
+    )(grads, received, *tables)
 
 
 def sums_kernel(query_ref, up_ref, conv_ref, out_ref):
@@ -380,26 +427,51 @@
     )(query, upstream, conv)
 
 
-def norm_kernel(channels, sums_ref, query_ref, up_ref, conv_ref, mixer_ref, dquery_ref, grad_ref):
+def norm_kernel(
+    channels,
+    own_ref,
+    other_ref,
+    query_ref,
+    up_ref,
+    conv_ref,
+    grad_ref,
+    mixer_hbm,
+    dquery_hbm,
+    mixer_ref,
+    dquery_ref,
+    sems,
+):
     tokens = query_ref.shape[0]
-    mean = sums_ref[0:1, :] / channels
-    dots = sums_ref[1:2, :] / channels
-    inverse_row = lax.rsqrt(mean + 1e-05)
-    slope_row = inverse_row * inverse_row * inverse_row * dots
-    inverse = jnp.broadcast_to(inverse_row, (LANES, tokens)).T
-    slope = jnp.broadcast_to(slope_row, (LANES, tokens)).T
-    for piece in range(conv_ref.shape[0]):
-        cols = slice(piece * LANES, (piece + 1) * LANES)
-        conv = conv_ref[piece].astype(jnp.float32)
-        query = query_ref[:, cols].astype(jnp.float32)
-        gated = query * conv
-        mixer_ref[:, cols] = (gated * inverse).astype(jnp.bfloat16)
-        dgated = inverse * up_ref[:, cols].astype(jnp.float32) - slope * gated
-        dquery_ref[:, cols] = (dgated * conv).astype(jnp.bfloat16)
-        grad_ref[piece] = (dgated * query).astype(jnp.bfloat16)
-
-
-def gate_norm(sums, query, upstream, conv, channels):
+    sums = (own_ref[...] + other_ref[...]) / channels
+    inverse_row = lax.rsqrt(sums[0:1, :] + 1e-05)
+    slope_row = inverse_row * inverse_row * inverse_row * sums[1:2, :]
+    inverses = jnp.broadcast_to(inverse_row, (LANES, tokens)).T
+    slopes = jnp.broadcast_to(slope_row, (LANES, tokens)).T
+    step = tokens // STEPS
+    copies = []
+    for i in range(STEPS):
+        row = slice(i * step, (i + 1) * step)
+        inverse, slope = inverses[row], slopes[row]
+        for piece in range(conv_ref.shape[0]):
+            cols = slice(piece * LANES, (piece + 1) * LANES)
+            conv = conv_ref[piece, row, :].astype(jnp.float32)
+            query = query_ref[row, cols].astype(jnp.float32)
+            gated = query * conv
+            mixer_ref[row, cols] = (gated * inverse).astype(jnp.bfloat16)
+            dgated = inverse * up_ref[row, cols].astype(jnp.float32) - slope * gated
+            dquery_ref[row, cols] = (dgated * conv).astype(jnp.bfloat16)
+            grad_ref[piece, row, :] = (dgated * query).astype(jnp.bfloat16)
+        copies += started(
+            [
+                pltpu.make_async_copy(source.at[row], target.at[row], sems.at[which, i])
+                for which, (source, target) in enumerate(((mixer_ref, mixer_hbm), (dquery_ref, dquery_hbm)))
+            ]
+        )
+    for copy in copies:
+        copy.wait()
+
+
+def gate_norm(own, other, query, upstream, conv, channels):
     tokens, width = query.shape
 
     def kernel(*refs):
@@ -408,36 +480,67 @@
     flat = jax.ShapeDtypeStruct((tokens, width), jnp.bfloat16)
     return pl.pallas_call(
         kernel,
-        in_specs=whole(4),
-        out_specs=whole(3),
-        out_shape=(flat, flat, jax.ShapeDtypeStruct(conv.shape, jnp.bfloat16)),
+        in_specs=whole(5),
+        out_specs=[
+            pl.BlockSpec(memory_space=pltpu.VMEM),
+            pl.BlockSpec(memory_space=pltpu.HBM),
+            pl.BlockSpec(memory_space=pltpu.HBM),
+        ],
+        out_shape=(jax.ShapeDtypeStruct(conv.shape, jnp.bfloat16), flat, flat),
+        scratch_shapes=[
+            pltpu.VMEM((tokens, width), jnp.bfloat16),
+            pltpu.VMEM((tokens, width), jnp.bfloat16),
+            pltpu.SemaphoreType.DMA((2, STEPS)),
+        ],
         name="norm",
         **params(8 * tokens * width, 12 * tokens * width),
-    )(sums, query, upstream, conv)
-
-
-def unpack_kernel(back_ref, key_ref, value_ref, dkey_ref, dvalue_ref, dtaps_ref):
+    )(own, other, query, upstream, conv)
+
+
+def unpack_kernel(
+    back_ref, key_ref, value_ref, dkey_hbm, dvalue_hbm, dtaps_hbm, dkey_ref, dvalue_ref, row_sems, tap_sems
+):
     tokens = key_ref.shape[0]
-    for piece in range(back_ref.shape[0]):
-        cols = slice(piece * LANES, (piece + 1) * LANES)
-        dmixed = back_ref[piece, :tokens, :].astype(jnp.float32)
-        dkey_ref[:, cols] = (dmixed * value_ref[:, cols].astype(jnp.float32)).astype(jnp.bfloat16)
-        dvalue_ref[:, cols] = (dmixed * key_ref[:, cols].astype(jnp.float32)).astype(jnp.bfloat16)
-        dtaps_ref[:, cols] = back_ref[piece, tokens:, :]
+    step = tokens // STEPS
+    rows = [slice(i * step, (i + 1) * step) for i in range(STEPS)]
+    cols = [slice(i * LANES, (i + 1) * LANES) for i in range(back_ref.shape[0])]
+    copies = started(
+        [
+            pltpu.make_async_copy(
+                back_ref.at[piece, pl.ds(tokens, tokens)], dtaps_hbm.at[:, col], tap_sems.at[piece]
+            )
+            for piece, col in enumerate(cols)
+        ]
+    )
+    for i, row in enumerate(rows):
+        for piece, col in enumerate(cols):
+            dmixed = back_ref[piece, row, :].astype(jnp.float32)
+            dkey_ref[row, col] = (dmixed * value_ref[row, col].astype(jnp.float32)).astype(jnp.bfloat16)
+            dvalue_ref[row, col] = (dmixed * key_ref[row, col].astype(jnp.float32)).astype(jnp.bfloat16)
+        copies += started(
+            [
+                pltpu.make_async_copy(source.at[row], target.at[row], row_sems.at[which, i])
+                for which, (source, target) in enumerate(((dkey_ref, dkey_hbm), (dvalue_ref, dvalue_hbm)))
+            ]
+        )
+    for copy in copies:
+        copy.wait()
 
 
 def unpack(back, key_proj, value_proj):
     tokens, width = key_proj.shape
-    pieces = width // LANES
-    step = 4 if pieces % 4 == 0 else pieces
-    wide = pl.BlockSpec((tokens, step * LANES), lambda i: (0, i))
     flat = jax.ShapeDtypeStruct((tokens, width), jnp.bfloat16)
     return pl.pallas_call(
         unpack_kernel,
-        grid=(pieces // step,),
-        in_specs=[pl.BlockSpec((step, 2 * tokens, LANES), lambda i: (i, 0, 0)), wide, wide],
-        out_specs=[wide] * 3,
+        in_specs=whole(3),
+        out_specs=[pl.BlockSpec(memory_space=pltpu.HBM)] * 3,
         out_shape=(flat, flat, flat),
+        scratch_shapes=[
+            pltpu.VMEM((tokens, width), jnp.bfloat16),
+            pltpu.VMEM((tokens, width), jnp.bfloat16),
+            pltpu.SemaphoreType.DMA((2, STEPS)),
+            pltpu.SemaphoreType.DMA((width // LANES,)),
+        ],
         name="unpack",
         **params(2 * tokens * width, 14 * tokens * width),
     )(back, key_proj, value_proj)
@@ -452,22 +555,22 @@
     width = query.shape[1] * lax.axis_size("tp")
     block = 2 * query.shape[0]
     scale = 1.0 / (math.sqrt(length) * block)
-    high, low = odd_tables(block)
-    tables = tuple(jnp.asarray(t) for t in (high, low, high.T.copy(), low.T.copy()))
+    tables = odd_tables(block)
     received = exchange(pack(key_proj, value_proj, filter_taps))
-    conv_cols, mix, tap = convolve(received, tables, scale)
-    conv = exchange(conv_cols)
-    sums = channel_total(token_sums(query, grad_out, conv))
-    mixer_out, dquery, grad_rows = gate_norm(sums, query, grad_out, conv, width)
-    back_cols = correlate(exchange(grad_rows), mix, tap, tables, scale)
-    dkey, dvalue, dtaps = unpack(exchange(back_cols), key_proj, value_proj)
+    conv = exchange(convolve(received, tables, scale))
+    own = token_sums(query, grad_out, conv)
+    other = lax.ppermute(own, "tp", [(0, 1), (1, 0)])
+    grads, mixer_out, dquery = gate_norm(own, other, query, grad_out, conv, width)
+    back = exchange(correlate(exchange(grads), received, tables, scale))
+    dkey, dvalue, dtaps = unpack(back, key_proj, value_proj)
     return (mixer_out, dquery, dkey, dvalue, dtaps)
 
 
 def per_device(query, key_proj, value_proj, filter_taps, grad_out):
     tokens, width = query.shape
     ring = lax.axis_size("ctx")
-    if width == ring * LANES and tokens == LANES and ring % 2 == 0:
+    pairs = lax.axis_size("tp") == 2
+    if pairs and width == ring * LANES and tokens == LANES and ring % 2 == 0:
         return per_device_kernels(query, key_proj, value_proj, filter_taps, grad_out)
     return per_device_plain(query, key_proj, value_proj, filter_taps, grad_out)
 

time: 124 us -> 116 us (0.935)
  local copies, waits for them, and re-layouts: 6.49 us -> 0.04 us
  blocking collectives: 103 us -> 100 us
  starting transfers between devices: 0 us -> 1.31 us
    unnamed x34 -> x12, local copies, waits for them, and re-layouts: 6.49 us -> 0.04 us
    psum x1 -> x0, blocking collectives: 3.78 us -> none  [channel_total(): return lax.psum(values, 'tp')]
    ppermute x0 -> x1, starting transfers between devices: none -> 1.31 us  [per_device_kernels(): other = lax.ppermute(own, 'tp', [(0, 1), (1, 0)])]
  transfers between devices with their start and end apart: 0 -> 1, of which waited for: 0 -> 1; matrix products, arithmetic and copies ran while one was open for 0% -> 0% of each run, Pallas kernels for 0% -> 0%
where the time goes in v2:
time: 116 us
  blocking collectives  100 us (86%)
  Pallas kernels  12.3 us (11%)
  starting transfers between devices  1.31 us (1%)
  waiting for transfers between devices  1.18 us (1%)
    all_to_all x4, blocking collectives, exchange(): lax.all_to_all(pieces, 'ctx', split_axis=0, concat_axis=0, tiled=True)  100 us
    pallas_call x1, Pallas kernels, correlate(): pl.pallas_call(kernel, in_specs=whole(4), out_specs=pl.BlockSpec(memory_s...  4.43 us
    pallas_call x1, Pallas kernels, pack(): pl.pallas_call(pack_kernel, in_specs=[pl.BlockSpec(memory_space=pltpu.HBM...  2.47 us
    pallas_call x1, Pallas kernels, convolve(): pl.pallas_call(kernel, in_specs=whole(3), out_specs=pl.BlockSpec(memory_s...  2.44 us
  transfers between devices with their start and end apart: 1, of which 1 were waited for; matrix products, arithmetic and copies ran while one was open for 0% of the time, Pallas kernels for 0%

profile of v2, /device:TPU:1, one launch (start us, length us, event | category | flops | bytes accessed | tf_op | source)
XLA Modules:
  0.0 115.7 jit_solution(3147479987497097580)
XLA Ops:
  0.6 2.5 %pack.1 = bf16[16,2,128,128]{3,2,1,0:T(8,128)(2,1)} custom-call(bf16[128,2048]{1,0:T(8,128)(2,1)} %key_ref.1, bf16[128,2048]{1,0:T(8,128)(2,1)} %value_ref.1, bf16[128,2048]{1,0:T(8,128)(2,1)} %taps_hbm.1), custom_call_target="tpu_custom_call" | custom-call | flops 262144 | bytes 2621440 | tf_op jit(solution)/shard_map/pack/pallas_call | solution.py:207
  3.1 0.0 copy-start.4
  3.1 0.0 copy-start.5
  3.1 32.7 %all_to_all.20.refs_0_.refs_1_ = bf16[16,256,128]{2,1,0:T(8,128)(2,1)S(1)} all-to-all(bf16[16,256,128]{2,1,0:T(8,128)(2,1)} %bitcast.1), channel_id=1, replica_groups=mesh['ctx'=16,'tp'=2] {'ctx'}, dimensions={0} | all-to-all | bytes 2097152 | tf_op jit(solution)/shard_map/all_to_all | solution.py:550
  35.8 0.0 copy-done.4
  35.8 0.0 copy-done.5
  35.8 2.4 %forward.1 = bf16[16,128,128]{2,1,0:T(8,128)(2,1)S(1)} custom-call(bf16[16,256,128]{2,1,0:T(8,128)(2,1)S(1)} %all_to_all.20.refs_0_.refs_1_, bf16[512,256]{1,0:T(8,128)(2,1)S(1)} %copy-done.5, bf16[256,512]{1,0:T(8,128)(2,1)S(1)} %copy-done.4), custom_call_target="tpu_custom_call" | custom-call | flops 805306368 | bytes 4194304 | tf_op jit(solution)/shard_map/forward/pallas_call | solution.py:367
  38.3 0.0 copy-start.2
  38.3 0.0 copy-start.3
  38.3 18.4 %all_to_all.21.conv_ref.refs_4_ = bf16[16,128,128]{2,1,0:T(8,128)(2,1)S(1)} all-to-all(bf16[16,128,128]{2,1,0:T(8,128)(2,1)S(1)} %forward.1), channel_id=1, replica_groups=mesh['ctx'=16,'tp'=2] {'ctx'}, dimensions={0} | all-to-all | bytes 1048576 | tf_op jit(solution)/shard_map/all_to_all | solution.py:550
  56.7 0.0 copy-done.2
  56.7 0.0 copy-done.3
  56.7 0.4 sums.1.refs_0_
  57.1 1.3 %collective-permute-start = (f32[2,128]{1,0:T(2,128)S(1)}, f32[2,128]{1,0:T(2,128)S(1)}, u32[]{:S(2)}, u32[]{:S(2)}) collective-permute-start(f32[2,128]{1,0:T(2,128)S(1)} %sums.1.refs_0_), channel_id=1, source_target_pairs={{0,1},{1,0},{2,3},{3,2},{4,5},{5,4},{6,7},{7,6},{8,9},{9,8},{10,11... | collective-permute-start | bytes 3080 | tf_op jit(solution)/shard_map/ppermute | solution.py:562
  58.4 1.2 %collective-permute-done.refs_1_ = f32[2,128]{1,0:T(2,128)S(1)} collective-permute-done((f32[2,128]{1,0:T(2,128)S(1)}, f32[2,128]{1,0:T(2,128)S(1)}, u32[]{:S(2)}, u32[]{:S(2)}) %collective-permute-start) | collective-permute-done | bytes 1056 | tf_op jit(solution)/shard_map/ppermute | solution.py:562
  59.6 1.3 %norm.1 = (bf16[16,128,128]{2,1,0:T(8,128)(2,1)S(1)}, bf16[128,2048]{1,0:T(8,128)(2,1)}, bf16[128,2048]{1,0:T(8,128)(2,1)}) custom-call(f32[2,128]{1,0:T(2,128)S(1)} %sums.1.refs_0_, f32[2,128]{1,0:T(2,128)S(1)} %collective-permute-done.refs_1_, bf16[128,2048]{1,0:T(8,128)(2,1)S(1)} %copy-done.2, bf16[128,2048]{1,0:T(8,128)(2,1)S(1)} %copy-done.3, ...), custom_call_target="tpu_custom_call" | custom-call | flops 2097152 | bytes 3145728 | tf_op jit(solution)/shard_map/norm/pallas_call | solution.py:481
  60.9 19.4 %all_to_all.22.refs_0_ = bf16[16,128,128]{2,1,0:T(8,128)(2,1)S(1)} all-to-all(bf16[16,128,128]{2,1,0:T(8,128)(2,1)S(1)} %get-tuple-element.13), channel_id=1, replica_groups=mesh['ctx'=16,'tp'=2] {'ctx'}, dimensions={0} | all-to-all | bytes 1048576 | tf_op jit(solution)/shard_map/all_to_all | solution.py:550
  80.3 4.4 %backward.1 = bf16[16,256,128]{2,1,0:T(8,128)(2,1)S(1)} custom-call(bf16[16,128,128]{2,1,0:T(8,128)(2,1)S(1)} %all_to_all.22.refs_0_, bf16[16,256,128]{2,1,0:T(8,128)(2,1)S(1)} %all_to_all.20.refs_0_.refs_1_, bf16[512,256]{1,0:T(8,128)(2,1)S(1)} %copy-done.5, bf16[256,512]{1,0:T(8,128)(2,1)S(1)} %copy-done.4), custom_call_target="tpu_custom_call" | custom-call | flops 1342177280 | bytes 4194304 | tf_op jit(solution)/shard_map/backward/pallas_call | solution.py:390
  84.7 0.0 copy-start
  84.7 0.0 copy-start.1
  84.7 29.6 %all_to_all.23.back_ref = bf16[16,256,128]{2,1,0:T(8,128)(2,1)S(1)} all-to-all(bf16[16,256,128]{2,1,0:T(8,128)(2,1)S(1)} %backward.1), channel_id=1, replica_groups=mesh['ctx'=16,'tp'=2] {'ctx'}, dimensions={0} | all-to-all | bytes 2097152 | tf_op jit(solution)/shard_map/all_to_all | solution.py:550
  114.3 0.0 copy-done
  114.3 0.0 copy-done.1
  114.3 1.3 %unpack.1 = (bf16[128,2048]{1,0:T(8,128)(2,1)}, bf16[128,2048]{1,0:T(8,128)(2,1)}, bf16[128,2048]{1,0:T(8,128)(2,1)}) custom-call(bf16[16,256,128]{2,1,0:T(8,128)(2,1)S(1)} %all_to_all.23.back_ref, bf16[128,2048]{1,0:T(8,128)(2,1)S(1)} %copy-done, bf16[128,2048]{1,0:T(8,128)(2,1)S(1)} %copy-done.1), custom_call_target="tpu_custom_call" | custom-call | flops 524288 | bytes 3670016 | tf_op jit(solution)/shard_map/unpack/pallas_call | solution.py:533
Async XLA Ops:
  3.1 32.7 %copy-start.4 = (bf16[256,512]{1,0:T(8,128)(2,1)S(1)}, bf16[256,512]{1,0:T(8,128)(2,1)}, u32[]{:S(2)}) copy-start(bf16[256,512]{1,0:T(8,128)(2,1)} %constant.5.clone.refs_2_.refs_3_) | copy-start | bytes 786436
  3.1 32.7 %copy-start.5 = (bf16[512,256]{1,0:T(8,128)(2,1)S(1)}, bf16[512,256]{1,0:T(8,128)(2,1)}, u32[]{:S(2)}) copy-start(bf16[512,256]{1,0:T(8,128)(2,1)} %constant.4.clone.refs_1_.refs_2_) | copy-start | bytes 786436
  38.3 18.4 %copy-start.2 = (bf16[128,2048]{1,0:T(8,128)(2,1)S(1)}, bf16[128,2048]{1,0:T(8,128)(2,1)}, u32[]{:S(2)}) copy-start(bf16[128,2048]{1,0:T(8,128)(2,1)} %refs_2_.3) | copy-start | bytes 1572868
  38.3 18.4 %copy-start.3 = (bf16[128,2048]{1,0:T(8,128)(2,1)S(1)}, bf16[128,2048]{1,0:T(8,128)(2,1)}, u32[]{:S(2)}) copy-start(bf16[128,2048]{1,0:T(8,128)(2,1)} %refs_3_.2) | copy-start | bytes 1572868
  57.1 2.5 %collective-permute-start = (f32[2,128]{1,0:T(2,128)S(1)}, f32[2,128]{1,0:T(2,128)S(1)}, u32[]{:S(2)}, u32[]{:S(2)}) collective-permute-start(f32[2,128]{1,0:T(2,128)S(1)} %sums.1.refs_0_), channel_id=1, source_target_pairs={{0,1},{1,0},{2,3},{3,2},{4,5},{5,4},{6,7},{7,6},{8,9},{9,8},{10,11... | collective-permute-start | bytes 3080 | tf_op jit(solution)/shard_map/ppermute | solution.py:562
  84.7 29.6 %copy-start = (bf16[128,2048]{1,0:T(8,128)(2,1)S(1)}, bf16[128,2048]{1,0:T(8,128)(2,1)}, u32[]{:S(2)}) copy-start(bf16[128,2048]{1,0:T(8,128)(2,1)} %key_ref.1) | copy-start | bytes 1572868
  84.7 29.6 %copy-start.1 = (bf16[128,2048]{1,0:T(8,128)(2,1)S(1)}, bf16[128,2048]{1,0:T(8,128)(2,1)}, u32[]{:S(2)}) copy-start(bf16[128,2048]{1,0:T(8,128)(2,1)} %value_ref.1) | copy-start | bytes 1572868

commit v3 on v2

--- a/solution.py
+++ b/solution.py
@@ -143,12 +143,14 @@
 LANES = 128
 ROWS = 16
 STEPS = 4
+GROUPS = 4
 
 
 def odd_tables(block):
     order = np.concatenate([np.arange(0, block, 2), np.arange(1, block, 2)])
     angle = np.pi * np.outer(2 * order + 1, np.arange(block)) / (2 * block)
-    forward = np.concatenate([np.cos(angle), -np.sin(angle)], axis=0).astype(jnp.bfloat16)
+    parts = np.stack([np.cos(angle), -np.sin(angle)]).reshape(2, GROUPS, block // GROUPS, block)
+    forward = parts.transpose(1, 0, 2, 3).reshape(2 * block, block).astype(jnp.bfloat16)
     return jnp.asarray(forward), jnp.asarray(forward.T.copy())
 
 
@@ -170,7 +172,7 @@
 
 
 def pack_kernel(
-    key_hbm, value_hbm, taps_hbm, out_hbm, key_ref, value_ref, stage_ref, in_sems, tap_sems, out_sems
+    key_hbm, value_hbm, taps_hbm, out_hbm, key_ref, value_ref, taps_ref, stage_ref, in_sems, out_sems
 ):
     pieces = stage_ref.shape[0]
     share = pieces // STEPS
@@ -181,11 +183,7 @@
             pltpu.make_async_copy(key_hbm.at[:, wide], key_ref.at[:, wide], in_sems.at[0, i]),
             pltpu.make_async_copy(value_hbm.at[:, wide], value_ref.at[:, wide], in_sems.at[1, i]),
         ]
-        for piece in range(i * share, (i + 1) * share):
-            col = slice(piece * LANES, (piece + 1) * LANES)
-            group.append(
-                pltpu.make_async_copy(taps_hbm.at[:, col], stage_ref.at[piece, 1], tap_sems.at[piece])
-            )
+        group.append(pltpu.make_async_copy(taps_hbm.at[:, wide], taps_ref.at[:, wide], in_sems.at[2, i]))
         loads.append(started(group))
     stores = []
     for i, group in enumerate(loads):
@@ -195,6 +193,7 @@
             col = slice(piece * LANES, (piece + 1) * LANES)
             product = key_ref[:, col].astype(jnp.float32) * value_ref[:, col].astype(jnp.float32)
             stage_ref[piece, 0] = product.astype(jnp.bfloat16)
+            stage_ref[piece, 1] = taps_ref[:, col]
         part = pl.ds(i * share, share)
         stores += started([pltpu.make_async_copy(stage_ref.at[part], out_hbm.at[part], out_sems.at[i])])
     for copy in stores:
@@ -212,9 +211,9 @@
         scratch_shapes=[
             pltpu.VMEM((tokens, width), jnp.bfloat16),
             pltpu.VMEM((tokens, width), jnp.bfloat16),
+            pltpu.VMEM((tokens, width), jnp.bfloat16),
             pltpu.VMEM((pieces, 2, tokens, LANES), jnp.bfloat16),
-            pltpu.SemaphoreType.DMA((2, STEPS)),
-            pltpu.SemaphoreType.DMA((pieces,)),
+            pltpu.SemaphoreType.DMA((3, STEPS)),
             pltpu.SemaphoreType.DMA((STEPS,)),
         ],
         name="pack",
@@ -223,136 +222,164 @@
     return packed.reshape(pieces, 2 * tokens, LANES)
 
 
-def block_columns(ref, offset, tokens, block):
+def transform(table_ref, spec_ref, group, in_ref, offset, tokens, tile):
+    block = table_ref.shape[1]
     per = block // tokens
     blocks = []
-    for b in range(ref.shape[0] // per):
-        parts = [ref[b * per + p, offset : offset + tokens, :] for p in range(per)]
+    for b in range(2):
+        parts = [
+            in_ref[(2 * tile + b) * per + p, offset : offset + tokens, :] for p in range(per)
+        ]
         blocks.append(jnp.concatenate(parts, axis=0))
-    return jnp.concatenate(blocks, axis=1)
-
-
-def to_spectrum(table_ref, columns):
-    return jnp.dot(table_ref[...], columns, preferred_element_type=jnp.float32)
-
-
-def store_signal(back_ref, spec_ref, out_ref, offset, tokens, scale):
+    columns = jnp.concatenate(blocks, axis=1)
+    size = spec_ref.shape[0]
+    rows = table_ref[group * size : (group + 1) * size, :]
+    lanes = pl.ds(tile * 2 * LANES, 2 * LANES)
+    spec_ref[:, lanes] = jnp.dot(rows, columns, preferred_element_type=jnp.float32)
+
+
+def restore(back_ref, acc_ref, out_ref, offset, tokens, scale, tile):
     per = back_ref.shape[0] // tokens
-    signal = jnp.dot(back_ref[...], spec_ref[...], preferred_element_type=jnp.float32)
+    lanes = slice(tile * 2 * LANES, (tile + 1) * 2 * LANES)
+    signal = jnp.dot(back_ref[...], acc_ref[:, lanes], preferred_element_type=jnp.float32)
     rounded = (signal * scale).astype(jnp.bfloat16)
-    for b in range(out_ref.shape[0] // per):
+    for b in range(2):
         for p in range(per):
-            out_ref[b * per + p, offset : offset + tokens, :] = rounded[
+            out_ref[(2 * tile + b) * per + p, offset : offset + tokens, :] = rounded[
                 p * tokens : (p + 1) * tokens, b * LANES : (b + 1) * LANES
             ]
 
 
-def each_tile(block, body):
-    half = block // 2
-    for sign, base in ((1.0, 0), (-1.0, half)):
-
-        def step(i, carry, sign=sign, base=base):
-            body(pl.multiple_of(base + i * ROWS, ROWS), sign)
-            return carry
-
-        lax.fori_loop(0, half // ROWS, step, 0)
-
-
-def tile_of(ref, row, b, block):
+def tile_of(ref, row, b):
+    half = ref.shape[0] // 2
     cols = slice(b * LANES, (b + 1) * LANES)
-    return (ref[pl.ds(row, ROWS), cols], ref[pl.ds(row + block, ROWS), cols])
-
-
-def put_tile(ref, row, b, block, real, imag):
+    return (ref[pl.ds(row, ROWS), cols], ref[pl.ds(row + half, ROWS), cols])
+
+
+def put_tile(ref, group, row, b, real, imag):
+    size = ref.shape[0] // GROUPS
     cols = slice(b * LANES, (b + 1) * LANES)
-    ref[pl.ds(row, ROWS), cols] = real.astype(ref.dtype)
-    ref[pl.ds(row + block, ROWS), cols] = imag.astype(ref.dtype)
+    ref[pl.ds(group * size + row, ROWS), cols] = real.astype(ref.dtype)
+    ref[pl.ds(group * size + size // 2 + row, ROWS), cols] = imag.astype(ref.dtype)
 
 
 def plus(total, term):
     return term if total is None else total + term
 
 
-def forward_products(mix_ref, tap_ref, acc_ref, block):
+def forward_products(mix_ref, tap_ref, acc_ref, group, row):
     count = mix_ref.shape[1] // LANES
-
-    def body(row, sign):
-        taps = [tile_of(tap_ref, row, b, block) for b in range(count)]
-        taps = [(r, i, r + i) for r, i in taps]
-        mixes = [tile_of(mix_ref, row, b, block) for b in range(count)]
-        mixes = [(r, i, r + i) for r, i in mixes]
-        before = None
-        for d in range(count):
-            first = second = third = None
-            for j in range(d + 1):
-                mr, mi, ms = mixes[j]
-                tr, ti, ts = taps[d - j]
-                first = plus(first, mr * tr)
-                second = plus(second, mi * ti)
-                third = plus(third, ms * ts)
-            real = first - second
-            imag = third - first - second
-            if before is None:
-                put_tile(acc_ref, row, d, block, real, imag)
-            elif sign > 0:
-                put_tile(acc_ref, row, d, block, real - before[1], imag + before[0])
-            else:
-                put_tile(acc_ref, row, d, block, real + before[1], imag - before[0])
-            before = (real, imag)
-
-    each_tile(block, body)
-
-
-def backward_products(grad_ref, other_ref, acc_ref, block):
+    taps = [tile_of(tap_ref, row, b) for b in range(count)]
+    taps = [(r, i, r + i) for r, i in taps]
+    mixes = [tile_of(mix_ref, row, b) for b in range(count)]
+    mixes = [(r, i, r + i) for r, i in mixes]
+    before = None
+    for d in range(count):
+        first = second = third = None
+        for j in range(d + 1):
+            mr, mi, ms = mixes[j]
+            tr, ti, ts = taps[d - j]
+            first = plus(first, mr * tr)
+            second = plus(second, mi * ti)
+            third = plus(third, ms * ts)
+        real = first - second
+        imag = third - first - second
+        if before is None:
+            put_tile(acc_ref, group, row, d, real, imag)
+        elif group < GROUPS // 2:
+            put_tile(acc_ref, group, row, d, real - before[1], imag + before[0])
+        else:
+            put_tile(acc_ref, group, row, d, real + before[1], imag - before[0])
+        before = (real, imag)
+
+
+def backward_products(grad_ref, other_ref, acc_ref, group, row):
     count = grad_ref.shape[1] // LANES
-
-    def body(row, sign):
-        others = [tile_of(other_ref, row, b, block) for b in range(count)]
-        others = [(r, i, r - i) for r, i in others]
-        grads = [tile_of(grad_ref, row, b, block) for b in range(count)]
-        grads = [(r, i, r + i) for r, i in grads]
-        after = None
-        for d in reversed(range(count)):
-            first = second = third = None
-            for k in range(count - d):
-                gr, gi, gs = grads[d + k]
-                ar, ai, ad = others[k]
-                first = plus(first, gr * ar)
-                second = plus(second, gi * ai)
-                third = plus(third, gs * ad)
-            real = first + second
-            imag = third - first + second
-            if after is None:
-                put_tile(acc_ref, row, d, block, real, imag)
-            elif sign > 0:
-                put_tile(acc_ref, row, d, block, real + after[1], imag - after[0])
-            else:
-                put_tile(acc_ref, row, d, block, real - after[1], imag + after[0])
-            after = (real, imag)
-
-    each_tile(block, body)
-
-
-def forward_kernel(scale, in_ref, table_ref, back_ref, out_ref, mix_ref, tap_ref, acc_ref):
-    block = table_ref.shape[1]
+    others = [tile_of(other_ref, row, b) for b in range(count)]
+    others = [(r, i, r - i) for r, i in others]
+    grads = [tile_of(grad_ref, row, b) for b in range(count)]
+    grads = [(r, i, r + i) for r, i in grads]
+    after = None
+    for d in reversed(range(count)):
+        first = second = third = None
+        for k in range(count - d):
+            gr, gi, gs = grads[d + k]
+            ar, ai, ad = others[k]
+            first = plus(first, gr * ar)
+            second = plus(second, gi * ai)
+            third = plus(third, gs * ad)
+        real = first + second
+        imag = third - first + second
+        if after is None:
+            put_tile(acc_ref, group, row, d, real, imag)
+        elif group < GROUPS // 2:
+            put_tile(acc_ref, group, row, d, real + after[1], imag - after[0])
+        else:
+            put_tile(acc_ref, group, row, d, real - after[1], imag + after[0])
+        after = (real, imag)
+
+
+def each_step(count, body):
+    for i in range(count):
+        body(i)
+
+
+def forward_kernel(scale, in_ref, table_ref, back_ref, out_ref, acc_ref, *spectra):
+    mixes, taps = spectra[:GROUPS], spectra[GROUPS:]
     tokens = out_ref.shape[1]
-    mix_ref[...] = to_spectrum(table_ref, block_columns(in_ref, 0, tokens, block))
-    tap_ref[...] = to_spectrum(table_ref, block_columns(in_ref, tokens, tokens, block))
-    forward_products(mix_ref, tap_ref, acc_ref, block)
-    store_signal(back_ref, acc_ref, out_ref, 0, tokens, scale)
-
-
-def backward_kernel(
-    scale, grad_in_ref, in_ref, table_ref, back_ref, out_ref, grad_ref, other_ref, acc_ref
-):
-    block = table_ref.shape[1]
+    tiles = acc_ref.shape[1] // (2 * LANES)
+
+    def transforms(group, tile):
+        transform(table_ref, mixes[group], group, in_ref, 0, tokens, tile)
+        transform(table_ref, taps[group], group, in_ref, tokens, tokens, tile)
+
+    for tile in range(tiles):
+        transforms(0, tile)
+    for group in range(GROUPS):
+
+        def step(i, group=group):
+            row = i * ROWS
+            if group + 1 < GROUPS:
+                transforms(group + 1, i)
+            forward_products(mixes[group], taps[group], acc_ref, group, row)
+
+        each_step(tiles, step)
+    for tile in range(tiles):
+        restore(back_ref, acc_ref, out_ref, 0, tokens, scale, tile)
+
+
+def backward_kernel(scale, grad_in_ref, in_ref, table_ref, back_ref, out_ref, mixed_ref, dtaps_ref, *spectra):
+    grads, taps, mixes = spectra[:GROUPS], spectra[GROUPS : 2 * GROUPS], spectra[2 * GROUPS :]
     tokens = grad_in_ref.shape[1]
-    grad_ref[...] = to_spectrum(table_ref, block_columns(grad_in_ref, 0, tokens, block))
-    for which in range(2):
-        columns = block_columns(in_ref, (1 - which) * tokens, tokens, block)
-        other_ref[...] = to_spectrum(table_ref, columns)
-        backward_products(grad_ref, other_ref, acc_ref, block)
-        store_signal(back_ref, acc_ref, out_ref, which * tokens, tokens, scale)
+    tiles = mixed_ref.shape[1] // (2 * LANES)
+
+    def transforms(group, tile):
+        transform(table_ref, grads[group], group, grad_in_ref, 0, tokens, tile)
+        transform(table_ref, taps[group], group, in_ref, tokens, tokens, tile)
+
+    for tile in range(tiles):
+        transforms(0, tile)
+    for group in range(GROUPS):
+
+        def step(i, group=group):
+            row = i * ROWS
+            if group + 1 < GROUPS:
+                transforms(group + 1, i)
+            transform(table_ref, mixes[group], group, in_ref, 0, tokens, i)
+            backward_products(grads[group], taps[group], mixed_ref, group, row)
+
+        each_step(tiles, step)
+    for group in range(GROUPS):
+
+        def step(i, group=group):
+            row = i * ROWS
+            if i == 0:
+                restore(back_ref, mixed_ref, out_ref, 0, tokens, scale, group)
+            backward_products(grads[group], mixes[group], dtaps_ref, group, row)
+
+        each_step(tiles, step)
+    for tile in range(tiles):
+        restore(back_ref, dtaps_ref, out_ref, tokens, tokens, scale, tile)
 
 
 def convolve(received, tables, scale):
@@ -369,11 +396,8 @@
         in_specs=whole(3),
         out_specs=pl.BlockSpec(memory_space=pltpu.VMEM),
         out_shape=jax.ShapeDtypeStruct((pieces, tokens, LANES), jnp.bfloat16),
-        scratch_shapes=[
-            pltpu.VMEM((freq, wide), jnp.float32),
-            pltpu.VMEM((freq, wide), jnp.float32),
-            pltpu.VMEM((freq, wide), jnp.bfloat16),
-        ],
+        scratch_shapes=[pltpu.VMEM((freq, wide), jnp.bfloat16)]
+        + [pltpu.VMEM((freq // GROUPS, wide), jnp.float32)] * (2 * GROUPS),
         name="forward",
         **params(6 * freq * block * wide, 8 * freq * wide),
     )(received, *tables)
@@ -392,11 +416,8 @@
         in_specs=whole(4),
         out_specs=pl.BlockSpec(memory_space=pltpu.VMEM),
         out_shape=jax.ShapeDtypeStruct((pieces, 2 * tokens, LANES), jnp.bfloat16),
-        scratch_shapes=[
-            pltpu.VMEM((freq, wide), jnp.float32),
-            pltpu.VMEM((freq, wide), jnp.float32),
-            pltpu.VMEM((freq, wide), jnp.bfloat16),
-        ],
+        scratch_shapes=[pltpu.VMEM((freq, wide), jnp.bfloat16)] * 2
+        + [pltpu.VMEM((freq // GROUPS, wide), jnp.float32)] * (3 * GROUPS),
         name="backward",
         **params(10 * freq * block * wide, 8 * freq * wide),
     )(grads, received, *tables)

time: 116 us -> 114 us (0.983)
  Pallas kernels: 12.3 us -> 10.7 us
where the time goes in v3:
time: 114 us
  blocking collectives  100 us (88%)
  Pallas kernels  10.7 us (9%)
  starting transfers between devices  1.3 us (1%)
  waiting for transfers between devices  1.19 us (1%)
    all_to_all x4, blocking collectives, exchange(): lax.all_to_all(pieces, 'ctx', split_axis=0, concat_axis=0, tiled=True)  100 us
    pallas_call x1, Pallas kernels, correlate(): pl.pallas_call(kernel, in_specs=whole(4), out_specs=pl.BlockSpec(memory_s...  3.51 us
    pallas_call x1, Pallas kernels, pack(): pl.pallas_call(pack_kernel, in_specs=[pl.BlockSpec(memory_space=pltpu.HBM...  2.35 us
  transfers between devices with their start and end apart: 1, of which 1 were waited for; matrix products, arithmetic and copies ran while one was open for 0% of the time, Pallas kernels for 0%

profile of v3, /device:TPU:1, one launch (start us, length us, event | category | flops | bytes accessed | tf_op | source)
XLA Modules:
  0.0 114.0 jit_solution(16798382014118687582)
XLA Ops:
  0.6 2.4 %pack.1 = bf16[16,2,128,128]{3,2,1,0:T(8,128)(2,1)} custom-call(bf16[128,2048]{1,0:T(8,128)(2,1)} %key_ref.1, bf16[128,2048]{1,0:T(8,128)(2,1)} %value_ref.1, bf16[128,2048]{1,0:T(8,128)(2,1)} %taps_hbm.1), custom_call_target="tpu_custom_call" | custom-call | flops 262144 | bytes 2621440 | tf_op jit(solution)/shard_map/pack/pallas_call | solution.py:206
  3.0 0.0 copy-start.4
  3.0 0.0 copy-start.5
  3.0 32.7 %all_to_all.20.refs_0_.refs_1_ = bf16[16,256,128]{2,1,0:T(8,128)(2,1)S(1)} all-to-all(bf16[16,256,128]{2,1,0:T(8,128)(2,1)} %bitcast.1), channel_id=1, replica_groups=mesh['ctx'=16,'tp'=2] {'ctx'}, dimensions={0} | all-to-all | bytes 2097152 | tf_op jit(solution)/shard_map/all_to_all | solution.py:571
  35.7 0.0 copy-done.4
  35.7 0.0 copy-done.5
  35.7 1.8 %forward.1 = bf16[16,128,128]{2,1,0:T(8,128)(2,1)S(1)} custom-call(bf16[16,256,128]{2,1,0:T(8,128)(2,1)S(1)} %all_to_all.20.refs_0_.refs_1_, bf16[512,256]{1,0:T(8,128)(2,1)S(1)} %copy-done.5, bf16[256,512]{1,0:T(8,128)(2,1)S(1)} %copy-done.4), custom_call_target="tpu_custom_call" | custom-call | flops 805306368 | bytes 4194304 | tf_op jit(solution)/shard_map/forward/pallas_call | solution.py:394
  37.6 0.0 copy-start.2
  37.6 0.0 copy-start.3
  37.6 18.4 %all_to_all.21.conv_ref.refs_4_ = bf16[16,128,128]{2,1,0:T(8,128)(2,1)S(1)} all-to-all(bf16[16,128,128]{2,1,0:T(8,128)(2,1)S(1)} %forward.1), channel_id=1, replica_groups=mesh['ctx'=16,'tp'=2] {'ctx'}, dimensions={0} | all-to-all | bytes 1048576 | tf_op jit(solution)/shard_map/all_to_all | solution.py:571
  56.0 0.0 copy-done.2
  56.0 0.0 copy-done.3
  56.0 0.4 sums.1.refs_0_
  56.4 1.3 %collective-permute-start = (f32[2,128]{1,0:T(2,128)S(1)}, f32[2,128]{1,0:T(2,128)S(1)}, u32[]{:S(2)}, u32[]{:S(2)}) collective-permute-start(f32[2,128]{1,0:T(2,128)S(1)} %sums.1.refs_0_), channel_id=1, source_target_pairs={{0,1},{1,0},{2,3},{3,2},{4,5},{5,4},{6,7},{7,6},{8,9},{9,8},{10,11... | collective-permute-start | bytes 3080 | tf_op jit(solution)/shard_map/ppermute | solution.py:583
  57.7 1.2 %collective-permute-done.refs_1_ = f32[2,128]{1,0:T(2,128)S(1)} collective-permute-done((f32[2,128]{1,0:T(2,128)S(1)}, f32[2,128]{1,0:T(2,128)S(1)}, u32[]{:S(2)}, u32[]{:S(2)}) %collective-permute-start) | collective-permute-done | bytes 1056 | tf_op jit(solution)/shard_map/ppermute | solution.py:583
  58.8 1.3 %norm.1 = (bf16[16,128,128]{2,1,0:T(8,128)(2,1)S(1)}, bf16[128,2048]{1,0:T(8,128)(2,1)}, bf16[128,2048]{1,0:T(8,128)(2,1)}) custom-call(f32[2,128]{1,0:T(2,128)S(1)} %sums.1.refs_0_, f32[2,128]{1,0:T(2,128)S(1)} %collective-permute-done.refs_1_, bf16[128,2048]{1,0:T(8,128)(2,1)S(1)} %copy-done.2, bf16[128,2048]{1,0:T(8,128)(2,1)S(1)} %copy-done.3, ...), custom_call_target="tpu_custom_call" | custom-call | flops 2097152 | bytes 3145728 | tf_op jit(solution)/shard_map/norm/pallas_call | solution.py:502
  60.2 19.4 %all_to_all.22.refs_0_ = bf16[16,128,128]{2,1,0:T(8,128)(2,1)S(1)} all-to-all(bf16[16,128,128]{2,1,0:T(8,128)(2,1)S(1)} %get-tuple-element.13), channel_id=1, replica_groups=mesh['ctx'=16,'tp'=2] {'ctx'}, dimensions={0} | all-to-all | bytes 1048576 | tf_op jit(solution)/shard_map/all_to_all | solution.py:571
  79.5 3.5 %backward.1 = bf16[16,256,128]{2,1,0:T(8,128)(2,1)S(1)} custom-call(bf16[16,128,128]{2,1,0:T(8,128)(2,1)S(1)} %all_to_all.22.refs_0_, bf16[16,256,128]{2,1,0:T(8,128)(2,1)S(1)} %all_to_all.20.refs_0_.refs_1_, bf16[512,256]{1,0:T(8,128)(2,1)S(1)} %copy-done.5, bf16[256,512]{1,0:T(8,128)(2,1)S(1)} %copy-done.4), custom_call_target="tpu_custom_call" | custom-call | flops 1342177280 | bytes 4194304 | tf_op jit(solution)/shard_map/backward/pallas_call | solution.py:414
  83.1 0.0 copy-start
  83.1 0.0 copy-start.1
  83.1 29.6 %all_to_all.23.back_ref = bf16[16,256,128]{2,1,0:T(8,128)(2,1)S(1)} all-to-all(bf16[16,256,128]{2,1,0:T(8,128)(2,1)S(1)} %backward.1), channel_id=1, replica_groups=mesh['ctx'=16,'tp'=2] {'ctx'}, dimensions={0} | all-to-all | bytes 2097152 | tf_op jit(solution)/shard_map/all_to_all | solution.py:571
  112.7 0.0 copy-done
  112.7 0.0 copy-done.1
  112.7 1.3 %unpack.1 = (bf16[128,2048]{1,0:T(8,128)(2,1)}, bf16[128,2048]{1,0:T(8,128)(2,1)}, bf16[128,2048]{1,0:T(8,128)(2,1)}) custom-call(bf16[16,256,128]{2,1,0:T(8,128)(2,1)S(1)} %all_to_all.23.back_ref, bf16[128,2048]{1,0:T(8,128)(2,1)S(1)} %copy-done, bf16[128,2048]{1,0:T(8,128)(2,1)S(1)} %copy-done.1), custom_call_target="tpu_custom_call" | custom-call | flops 524288 | bytes 3670016 | tf_op jit(solution)/shard_map/unpack/pallas_call | solution.py:554
Async XLA Ops:
  3.0 32.7 %copy-start.4 = (bf16[256,512]{1,0:T(8,128)(2,1)S(1)}, bf16[256,512]{1,0:T(8,128)(2,1)}, u32[]{:S(2)}) copy-start(bf16[256,512]{1,0:T(8,128)(2,1)} %constant.5.clone.refs_2_.refs_3_) | copy-start | bytes 786436
  3.0 32.7 %copy-start.5 = (bf16[512,256]{1,0:T(8,128)(2,1)S(1)}, bf16[512,256]{1,0:T(8,128)(2,1)}, u32[]{:S(2)}) copy-start(bf16[512,256]{1,0:T(8,128)(2,1)} %constant.4.clone.refs_1_.refs_2_) | copy-start | bytes 786436
  37.6 18.4 %copy-start.2 = (bf16[128,2048]{1,0:T(8,128)(2,1)S(1)}, bf16[128,2048]{1,0:T(8,128)(2,1)}, u32[]{:S(2)}) copy-start(bf16[128,2048]{1,0:T(8,128)(2,1)} %refs_2_.3) | copy-start | bytes 1572868
  37.6 18.4 %copy-start.3 = (bf16[128,2048]{1,0:T(8,128)(2,1)S(1)}, bf16[128,2048]{1,0:T(8,128)(2,1)}, u32[]{:S(2)}) copy-start(bf16[128,2048]{1,0:T(8,128)(2,1)} %refs_3_.2) | copy-start | bytes 1572868
  56.4 2.5 %collective-permute-start = (f32[2,128]{1,0:T(2,128)S(1)}, f32[2,128]{1,0:T(2,128)S(1)}, u32[]{:S(2)}, u32[]{:S(2)}) collective-permute-start(f32[2,128]{1,0:T(2,128)S(1)} %sums.1.refs_0_), channel_id=1, source_target_pairs={{0,1},{1,0},{2,3},{3,2},{4,5},{5,4},{6,7},{7,6},{8,9},{9,8},{10,11... | collective-permute-start | bytes 3080 | tf_op jit(solution)/shard_map/ppermute | solution.py:583
  83.1 29.6 %copy-start = (bf16[128,2048]{1,0:T(8,128)(2,1)S(1)}, bf16[128,2048]{1,0:T(8,128)(2,1)}, u32[]{:S(2)}) copy-start(bf16[128,2048]{1,0:T(8,128)(2,1)} %key_ref.1) | copy-start | bytes 1572868
  83.1 29.6 %copy-start.1 = (bf16[128,2048]{1,0:T(8,128)(2,1)S(1)}, bf16[128,2048]{1,0:T(8,128)(2,1)}, u32[]{:S(2)}) copy-start(bf16[128,2048]{1,0:T(8,128)(2,1)} %value_ref.1) | copy-start | bytes 1572868

commit v4 on v3

--- a/solution.py
+++ b/solution.py
@@ -348,10 +348,21 @@
         restore(back_ref, acc_ref, out_ref, 0, tokens, scale, tile)
 
 
-def backward_kernel(scale, grad_in_ref, in_ref, table_ref, back_ref, out_ref, mixed_ref, dtaps_ref, *spectra):
+def backward_kernel(
+    scale, grad_in_ref, in_ref, table_ref, back_ref, out_hbm, out_ref, sems, mixed_ref, dtaps_ref, *spectra
+):
     grads, taps, mixes = spectra[:GROUPS], spectra[GROUPS : 2 * GROUPS], spectra[2 * GROUPS :]
     tokens = grad_in_ref.shape[1]
     tiles = mixed_ref.shape[1] // (2 * LANES)
+
+    copies = []
+
+    def send(offset, which, tile):
+        share = out_ref.shape[0] // tiles
+        part = (pl.ds(tile * share, share), pl.ds(offset, tokens))
+        copies.extend(
+            started([pltpu.make_async_copy(out_ref.at[part], out_hbm.at[part], sems.at[which, tile])])
+        )
 
     def transforms(group, tile):
         transform(table_ref, grads[group], group, grad_in_ref, 0, tokens, tile)
@@ -375,11 +386,15 @@
             row = i * ROWS
             if i == 0:
                 restore(back_ref, mixed_ref, out_ref, 0, tokens, scale, group)
+                send(0, 0, group)
             backward_products(grads[group], mixes[group], dtaps_ref, group, row)
 
         each_step(tiles, step)
     for tile in range(tiles):
         restore(back_ref, dtaps_ref, out_ref, tokens, tokens, scale, tile)
+        send(tokens, 1, tile)
+    for copy in copies:
+        copy.wait()
 
 
 def convolve(received, tables, scale):
@@ -414,9 +429,13 @@
     return pl.pallas_call(
         kernel,
         in_specs=whole(4),
-        out_specs=pl.BlockSpec(memory_space=pltpu.VMEM),
+        out_specs=pl.BlockSpec(memory_space=pltpu.HBM),
         out_shape=jax.ShapeDtypeStruct((pieces, 2 * tokens, LANES), jnp.bfloat16),
-        scratch_shapes=[pltpu.VMEM((freq, wide), jnp.bfloat16)] * 2
+        scratch_shapes=[
+            pltpu.VMEM((pieces, 2 * tokens, LANES), jnp.bfloat16),
+            pltpu.SemaphoreType.DMA((2, GROUPS)),
+        ]
+        + [pltpu.VMEM((freq, wide), jnp.bfloat16)] * 2
         + [pltpu.VMEM((freq // GROUPS, wide), jnp.float32)] * (3 * GROUPS),
         name="backward",
         **params(10 * freq * block * wide, 8 * freq * wide),
@@ -448,73 +467,87 @@
     )(query, upstream, conv)
 
 
-def norm_kernel(
-    channels,
-    own_ref,
-    other_ref,
-    query_ref,
-    up_ref,
-    conv_ref,
-    grad_ref,
-    mixer_hbm,
-    dquery_hbm,
-    mixer_ref,
-    dquery_ref,
-    sems,
-):
-    tokens = query_ref.shape[0]
+def columns_of(channels, own_ref, other_ref, tokens):
     sums = (own_ref[...] + other_ref[...]) / channels
     inverse_row = lax.rsqrt(sums[0:1, :] + 1e-05)
     slope_row = inverse_row * inverse_row * inverse_row * sums[1:2, :]
-    inverses = jnp.broadcast_to(inverse_row, (LANES, tokens)).T
-    slopes = jnp.broadcast_to(slope_row, (LANES, tokens)).T
-    step = tokens // STEPS
-    copies = []
-    for i in range(STEPS):
-        row = slice(i * step, (i + 1) * step)
-        inverse, slope = inverses[row], slopes[row]
-        for piece in range(conv_ref.shape[0]):
-            cols = slice(piece * LANES, (piece + 1) * LANES)
-            conv = conv_ref[piece, row, :].astype(jnp.float32)
-            query = query_ref[row, cols].astype(jnp.float32)
-            gated = query * conv
-            mixer_ref[row, cols] = (gated * inverse).astype(jnp.bfloat16)
-            dgated = inverse * up_ref[row, cols].astype(jnp.float32) - slope * gated
-            dquery_ref[row, cols] = (dgated * conv).astype(jnp.bfloat16)
-            grad_ref[piece, row, :] = (dgated * query).astype(jnp.bfloat16)
-        copies += started(
-            [
-                pltpu.make_async_copy(source.at[row], target.at[row], sems.at[which, i])
-                for which, (source, target) in enumerate(((mixer_ref, mixer_hbm), (dquery_ref, dquery_hbm)))
-            ]
-        )
-    for copy in copies:
-        copy.wait()
-
-
-def gate_norm(own, other, query, upstream, conv, channels):
+    inverse = jnp.broadcast_to(inverse_row, (LANES, tokens)).T
+    slope = jnp.broadcast_to(slope_row, (LANES, tokens)).T
+    return inverse, slope
+
+
+def grad_kernel(channels, own_ref, other_ref, query_ref, up_ref, conv_ref, grad_ref):
+    inverse, slope = columns_of(channels, own_ref, other_ref, query_ref.shape[0])
+    for piece in range(conv_ref.shape[0]):
+        cols = slice(piece * LANES, (piece + 1) * LANES)
+        query = query_ref[:, cols].astype(jnp.float32)
+        gated = query * conv_ref[piece].astype(jnp.float32)
+        dgated = inverse * up_ref[:, cols].astype(jnp.float32) - slope * gated
+        grad_ref[piece] = (dgated * query).astype(jnp.bfloat16)
+
+
+def norm_kernel(channels, own_ref, other_ref, query_ref, up_ref, conv_ref, mixer_ref, dquery_ref):
+    inverse, slope = columns_of(channels, own_ref, other_ref, query_ref.shape[0])
+    for piece in range(conv_ref.shape[0]):
+        cols = slice(piece * LANES, (piece + 1) * LANES)
+        conv = conv_ref[piece].astype(jnp.float32)
+        gated = query_ref[:, cols].astype(jnp.float32) * conv
+        mixer_ref[:, cols] = (gated * inverse).astype(jnp.bfloat16)
+        dgated = inverse * up_ref[:, cols].astype(jnp.float32) - slope * gated
+        dquery_ref[:, cols] = (dgated * conv).astype(jnp.bfloat16)
+
+
+def gate_grad(own, other, query, upstream, conv, channels):
     tokens, width = query.shape
 
     def kernel(*refs):
-        norm_kernel(channels, *refs)
-
-    flat = jax.ShapeDtypeStruct((tokens, width), jnp.bfloat16)
+        grad_kernel(channels, *refs)
+
     return pl.pallas_call(
         kernel,
         in_specs=whole(5),
-        out_specs=[
-            pl.BlockSpec(memory_space=pltpu.VMEM),
-            pl.BlockSpec(memory_space=pltpu.HBM),
-            pl.BlockSpec(memory_space=pltpu.HBM),
-        ],
-        out_shape=(jax.ShapeDtypeStruct(conv.shape, jnp.bfloat16), flat, flat),
-        scratch_shapes=[
-            pltpu.VMEM((tokens, width), jnp.bfloat16),
-            pltpu.VMEM((tokens, width), jnp.bfloat16),
-            pltpu.SemaphoreType.DMA((2, STEPS)),
-        ],
+        out_specs=pl.BlockSpec(memory_space=pltpu.VMEM),
+        out_shape=jax.ShapeDtypeStruct(conv.shape, jnp.bfloat16),
+        name="gate_grad",
+        **params(5 * tokens * width, 8 * tokens * width),
+    )(own, other, query, upstream, conv)
+
+
+def gate_norm(own, other, query, upstream, conv, channels):
+    tokens, width = query.shape
+    step = tokens // 4
+
+    def kernel(own_ref, other_ref, query_ref, up_ref, conv_ref, mixer_ref, dquery_ref, inv_ref, slope_ref):
+        i = pl.program_id(0)
+
+        @pl.when(i == 0)
+        def _():
+            inverse, slope = columns_of(channels, own_ref, other_ref, tokens)
+            inv_ref[...] = inverse
+            slope_ref[...] = slope
+
+        rows = pl.ds(pl.multiple_of(i * step, step), step)
+        inverse, slope = inv_ref[rows, :], slope_ref[rows, :]
+        for piece in range(conv_ref.shape[0]):
+            cols = slice(piece * LANES, (piece + 1) * LANES)
+            conv = conv_ref[piece].astype(jnp.float32)
+            gated = query_ref[:, cols].astype(jnp.float32) * conv
+            mixer_ref[:, cols] = (gated * inverse).astype(jnp.bfloat16)
+            dgated = inverse * up_ref[:, cols].astype(jnp.float32) - slope * gated
+            dquery_ref[:, cols] = (dgated * conv).astype(jnp.bfloat16)
+
+    flat = jax.ShapeDtypeStruct((tokens, width), jnp.bfloat16)
+    wide = pl.BlockSpec((step, width), lambda i: (i, 0))
+    small = pl.BlockSpec((2, tokens), lambda i: (0, 0))
+    return pl.pallas_call(
+        kernel,
+        grid=(4,),
+        in_specs=[small, small, wide, wide, pl.BlockSpec((conv.shape[0], step, LANES), lambda i: (0, i, 0))],
+        out_specs=[wide, wide],
+        out_shape=(flat, flat),
+        scratch_shapes=[pltpu.VMEM((tokens, LANES), jnp.float32)] * 2,
         name="norm",
-        **params(8 * tokens * width, 12 * tokens * width),
+        **params(6 * tokens * width, 10 * tokens * width, 60),
     )(own, other, query, upstream, conv)
 
 
@@ -581,8 +614,9 @@
     conv = exchange(convolve(received, tables, scale))
     own = token_sums(query, grad_out, conv)
     other = lax.ppermute(own, "tp", [(0, 1), (1, 0)])
-    grads, mixer_out, dquery = gate_norm(own, other, query, grad_out, conv, width)
-    back = exchange(correlate(exchange(grads), received, tables, scale))
+    grads = exchange(gate_grad(own, other, query, grad_out, conv, width))
+    mixer_out, dquery = gate_norm(own, other, query, grad_out, conv, width)
+    back = exchange(correlate(grads, received, tables, scale))
     dkey, dvalue, dtaps = unpack(back, key_proj, value_proj)
     return (mixer_out, dquery, dkey, dvalue, dtaps)
 
@@ -591,7 +625,7 @@
     tokens, width = query.shape
     ring = lax.axis_size("ctx")
     pairs = lax.axis_size("tp") == 2
-    if pairs and width == ring * LANES and tokens == LANES and ring % 2 == 0:
+    if pairs and width == ring * LANES and tokens == LANES and ring == 4 * GROUPS:
         return per_device_kernels(query, key_proj, value_proj, filter_taps, grad_out)
     return per_device_plain(query, key_proj, value_proj, filter_taps, grad_out)
 

time: 114 us -> 113 us (level)
  blocking collectives: 100 us -> 70.5 us
  waiting for transfers between devices: 1.19 us -> 20.5 us
  starting transfers between devices: 1.3 us -> 5.75 us
  Pallas kernels: 10.7 us -> 14.4 us
    all_to_all x4 -> x3, blocking collectives: 100 us -> 70.5 us  [exchange(): lax.all_to_all(pieces, 'ctx', split_axis=0, concat_axis=0, tiled=True)]
    all_to_all x0 -> x1, waiting for transfers between devices: none -> 19.3 us  [exchange(): lax.all_to_all(pieces, 'ctx', split_axis=0, concat_axis=0, tiled=True)]
    all_to_all x0 -> x1, starting transfers between devices: none -> 4.45 us  [exchange(): lax.all_to_all(pieces, 'ctx', split_axis=0, concat_axis=0, tiled=True)]
    pallas_call x1 -> x2, Pallas kernels: 1.3 us -> 4.25 us  [the longest x1 3.89 us: gate_norm(): pl.pallas_call(kernel, grid=(4,), in_specs=[small, small, wide, wide, pl....]
  transfers between devices with their start and end apart: 1 -> 2, of which waited for: 1 -> 2; matrix products, arithmetic and copies ran while one was open for 0% -> 0% of each run, Pallas kernels for 0% -> 3%
where the time goes in v4:
time: 113 us; the launch traced here: 112 us
  blocking collectives  70.5 us (62%)
  waiting for transfers between devices  20.5 us (18%)
  Pallas kernels  14.4 us (13%)
  starting transfers between devices  5.75 us (5%)
    all_to_all x3, blocking collectives, exchange(): lax.all_to_all(pieces, 'ctx', split_axis=0, concat_axis=0, tiled=True)  70.5 us
    all_to_all x1, waiting for transfers between devices, exchange(): lax.all_to_all(pieces, 'ctx', split_axis=0, concat_axis=0, tiled=True)  19.3 us
    all_to_all x1, starting transfers between devices, exchange(): lax.all_to_all(pieces, 'ctx', split_axis=0, concat_axis=0, tiled=True)  4.45 us
    pallas_call x1, Pallas kernels, correlate(): pl.pallas_call(kernel, in_specs=whole(4), out_specs=pl.BlockSpec(memory_s...  4.25 us
    pallas_call x1, Pallas kernels, gate_norm(): pl.pallas_call(kernel, grid=(4,), in_specs=[small, small, wide, wide, pl....  3.89 us
    pallas_call x1, Pallas kernels, pack(): pl.pallas_call(pack_kernel, in_specs=[pl.BlockSpec(memory_space=pltpu.HBM...  2.36 us
  transfers between devices with their start and end apart: 2, of which 2 were waited for; matrix products, arithmetic and copies ran while one was open for 0% of the time, Pallas kernels for 3%

profile of v4, /device:TPU:1, one launch (start us, length us, event | category | flops | bytes accessed | tf_op | source)
XLA Modules:
  0.0 112.0 jit_solution(12476236372776753787)
XLA Ops:
  0.6 2.4 %pack.1 = bf16[16,2,128,128]{3,2,1,0:T(8,128)(2,1)} custom-call(bf16[128,2048]{1,0:T(8,128)(2,1)} %key_ref.1, bf16[128,2048]{1,0:T(8,128)(2,1)} %value_ref.1, bf16[128,2048]{1,0:T(8,128)(2,1)} %taps_hbm.1), custom_call_target="tpu_custom_call" | custom-call | flops 262144 | bytes 2621440 | tf_op jit(solution)/shard_map/pack/pallas_call | solution.py:206
  3.0 0.0 copy-start.7
  3.0 0.0 copy-start.8
  3.0 32.7 %all_to_all.20.refs_0_.refs_1_ = bf16[16,256,128]{2,1,0:T(8,128)(2,1)S(1)} all-to-all(bf16[16,256,128]{2,1,0:T(8,128)(2,1)} %bitcast.1), channel_id=1, replica_groups=mesh['ctx'=16,'tp'=2] {'ctx'}, dimensions={0} | all-to-all | bytes 2097152 | tf_op jit(solution)/shard_map/all_to_all | solution.py:604
  35.7 1.8 %forward.1 = bf16[16,128,128]{2,1,0:T(8,128)(2,1)S(1)} custom-call(bf16[16,256,128]{2,1,0:T(8,128)(2,1)S(1)} %all_to_all.20.refs_0_.refs_1_, bf16[512,256]{1,0:T(8,128)(2,1)S(1)} %copy-done.7, bf16[256,512]{1,0:T(8,128)(2,1)S(1)} %copy-done.8), custom_call_target="tpu_custom_call" | custom-call | flops 805306368 | bytes 4194304 | tf_op jit(solution)/shard_map/forward/pallas_call | solution.py:409
  37.6 0.0 copy-start.1
  37.6 0.0 copy-start.2
  37.6 18.4 %all_to_all.21.conv_ref.refs_4_ = bf16[16,128,128]{2,1,0:T(8,128)(2,1)S(1)} all-to-all(bf16[16,128,128]{2,1,0:T(8,128)(2,1)S(1)} %forward.1), channel_id=1, replica_groups=mesh['ctx'=16,'tp'=2] {'ctx'}, dimensions={0} | all-to-all | bytes 1048576 | tf_op jit(solution)/shard_map/all_to_all | solution.py:604
  56.0 0.0 copy-done.1
  56.0 0.4 sums.1.own_ref.refs_0_
  56.4 0.0 copy-start.5
  56.4 1.3 %collective-permute-start = (f32[2,128]{1,0:T(2,128)S(1)}, f32[2,128]{1,0:T(2,128)S(1)}, u32[]{:S(2)}, u32[]{:S(2)}) collective-permute-start(f32[2,128]{1,0:T(2,128)S(1)} %sums.1.own_ref.refs_0_), channel_id=1, source_target_pairs={{0,1},{1,0},{2,3},{3,2},{4,5},{5,4},{6,7},{7,6},{8,9},{9,8},{10,11... | collective-permute-start | bytes 3080 | tf_op jit(solution)/shard_map/ppermute | solution.py:616
  57.7 1.2 %collective-permute-done.other_ref.refs_1_ = f32[2,128]{1,0:T(2,128)S(1)} collective-permute-done((f32[2,128]{1,0:T(2,128)S(1)}, f32[2,128]{1,0:T(2,128)S(1)}, u32[]{:S(2)}, u32[]{:S(2)}) %collective-permute-start) | collective-permute-done | bytes 1056 | tf_op jit(solution)/shard_map/ppermute | solution.py:616
  58.9 0.0 copy-done
  58.9 0.4 gate_grad.1
  59.2 0.2 copy-done.6
  59.4 19.4 %all_to_all.22.refs_0_ = bf16[16,128,128]{2,1,0:T(8,128)(2,1)S(1)} all-to-all(bf16[16,128,128]{2,1,0:T(8,128)(2,1)S(1)} %gate_grad.1), channel_id=1, replica_groups=mesh['ctx'=16,'tp'=2] {'ctx'}, dimensions={0} | all-to-all | bytes 1048576 | tf_op jit(solution)/shard_map/all_to_all | solution.py:604
  78.8 4.3 %backward.1 = bf16[16,256,128]{2,1,0:T(8,128)(2,1)} custom-call(bf16[16,128,128]{2,1,0:T(8,128)(2,1)S(1)} %all_to_all.22.refs_0_, bf16[16,256,128]{2,1,0:T(8,128)(2,1)S(1)} %all_to_all.20.refs_0_.refs_1_, bf16[512,256]{1,0:T(8,128)(2,1)S(1)} %copy-done.7, bf16[256,512]{1,0:T(8,128)(2,1)S(1)} %copy-done.8), custom_call_target="tpu_custom_call" | custom-call | flops 1342177280 | bytes 4194304 | tf_op jit(solution)/shard_map/backward/pallas_call | solution.py:429
  83.1 4.4 %all-to-all-start.3 = ((bf16[16,256,128]{2,1,0:T(8,128)(2,1)}), bf16[16,256,128]{2,1,0:T(8,128)(2,1)S(1)}, u32[]{:S(2)}, u32[]{:S(2)}) async-start(bf16[16,256,128]{2,1,0:T(8,128)(2,1)} %backward.1), calls=%async_computation.3 | async-start | bytes 2097152 | tf_op jit(solution)/shard_map/all_to_all | solution.py:604
  87.5 0.0 copy-start.4
  87.5 3.9 %norm.1 = (bf16[128,2048]{1,0:T(8,128)(2,1)}, bf16[128,2048]{1,0:T(8,128)(2,1)}) custom-call(f32[2,128]{1,0:T(2,128)} %copy-done.5, f32[2,128]{1,0:T(2,128)} %copy-done.6, bf16[128,2048]{1,0:T(8,128)(2,1)} %refs_2_.3, bf16[128,2048]{1,0:T(8,128)(2,1)} %refs_3_.2, bf16[16,128,128]{2,1,0:T(8,128)(2,1)} %copy-done), custom_call_target="tpu_custom_call" | custom-call | flops 1572864 | bytes 2621440 | tf_op jit(solution)/shard_map/norm/pallas_call | solution.py:542
  91.4 19.3 %all-to-all-done.3.back_ref = bf16[16,256,128]{2,1,0:T(8,128)(2,1)S(1)} async-done(((bf16[16,256,128]{2,1,0:T(8,128)(2,1)}), bf16[16,256,128]{2,1,0:T(8,128)(2,1)S(1)}, u32[]{:S(2)}, u32[]{:S(2)}) %all-to-all-start.3) | async-done | bytes 1048608 | tf_op jit(solution)/shard_map/all_to_all | solution.py:604
  110.7 0.0 copy-done.3
  110.7 1.3 %unpack.1 = (bf16[128,2048]{1,0:T(8,128)(2,1)}, bf16[128,2048]{1,0:T(8,128)(2,1)}, bf16[128,2048]{1,0:T(8,128)(2,1)}) custom-call(bf16[16,256,128]{2,1,0:T(8,128)(2,1)S(1)} %all-to-all-done.3.back_ref, bf16[128,2048]{1,0:T(8,128)(2,1)S(1)} %copy-done.3, bf16[128,2048]{1,0:T(8,128)(2,1)S(1)} %copy-done.4), custom_call_target="tpu_custom_call" | custom-call | flops 524288 | bytes 3670016 | tf_op jit(solution)/shard_map/unpack/pallas_call | solution.py:587
  (8 shorter events, 0.0 us)
Async XLA Ops:
  3.0 32.7 %copy-start.7 = (bf16[512,256]{1,0:T(8,128)(2,1)S(1)}, bf16[512,256]{1,0:T(8,128)(2,1)}, u32[]{:S(2)}) copy-start(bf16[512,256]{1,0:T(8,128)(2,1)} %constant.4.clone.refs_1_.refs_2_) | copy-start | bytes 786436
  3.0 32.7 %copy-start.8 = (bf16[256,512]{1,0:T(8,128)(2,1)S(1)}, bf16[256,512]{1,0:T(8,128)(2,1)}, u32[]{:S(2)}) copy-start(bf16[256,512]{1,0:T(8,128)(2,1)} %constant.5.clone.refs_2_.refs_3_) | copy-start | bytes 786436
  37.6 18.4 %copy-start.1 = (bf16[128,2048]{1,0:T(8,128)(2,1)S(1)}, bf16[128,2048]{1,0:T(8,128)(2,1)}, u32[]{:S(2)}) copy-start(bf16[128,2048]{1,0:T(8,128)(2,1)} %refs_2_.3) | copy-start | bytes 1572868
  37.6 18.4 %copy-start.2 = (bf16[128,2048]{1,0:T(8,128)(2,1)S(1)}, bf16[128,2048]{1,0:T(8,128)(2,1)}, u32[]{:S(2)}) copy-start(bf16[128,2048]{1,0:T(8,128)(2,1)} %refs_3_.2) | copy-start | bytes 1572868
  56.0 2.9 %copy-start = (bf16[16,128,128]{2,1,0:T(8,128)(2,1)}, bf16[16,128,128]{2,1,0:T(8,128)(2,1)S(1)}, u32[]{:S(2)}) copy-start(bf16[16,128,128]{2,1,0:T(8,128)(2,1)S(1)} %all_to_all.21.conv_ref.refs_4_) | copy-start | bytes 1572868
  56.4 2.9 %copy-start.5 = (f32[2,128]{1,0:T(2,128)}, f32[2,128]{1,0:T(2,128)S(1)}, u32[]{:S(2)}) copy-start(f32[2,128]{1,0:T(2,128)S(1)} %sums.1.own_ref.refs_0_) | copy-start | bytes 3076
  56.4 2.5 %collective-permute-start = (f32[2,128]{1,0:T(2,128)S(1)}, f32[2,128]{1,0:T(2,128)S(1)}, u32[]{:S(2)}, u32[]{:S(2)}) collective-permute-start(f32[2,128]{1,0:T(2,128)S(1)} %sums.1.own_ref.refs_0_), channel_id=1, source_target_pairs={{0,1},{1,0},{2,3},{3,2},{4,5},{5,4},{6,7},{7,6},{8,9},{9,8},{10,11... | collective-permute-start | bytes 3080 | tf_op jit(solution)/shard_map/ppermute | solution.py:616
  58.9 0.6 copy-start.6
  83.1 27.6 %all-to-all-start.3 = ((bf16[16,256,128]{2,1,0:T(8,128)(2,1)}), bf16[16,256,128]{2,1,0:T(8,128)(2,1)S(1)}, u32[]{:S(2)}, u32[]{:S(2)}) async-start(bf16[16,256,128]{2,1,0:T(8,128)(2,1)} %backward.1), calls=%async_computation.3 | async-start | bytes 2097152 | tf_op jit(solution)/shard_map/all_to_all | solution.py:604
  87.5 23.2 %copy-start.3 = (bf16[128,2048]{1,0:T(8,128)(2,1)S(1)}, bf16[128,2048]{1,0:T(8,128)(2,1)}, u32[]{:S(2)}) copy-start(bf16[128,2048]{1,0:T(8,128)(2,1)} %key_ref.1) | copy-start | bytes 1572868
  87.5 23.2 %copy-start.4 = (bf16[128,2048]{1,0:T(8,128)(2,1)S(1)}, bf16[128,2048]{1,0:T(8,128)(2,1)}, u32[]{:S(2)}) copy-start(bf16[128,2048]{1,0:T(8,128)(2,1)} %value_ref.1) | copy-start | bytes 1572868

commit v5 on v4

--- a/solution.py
+++ b/solution.py
@@ -150,8 +150,10 @@
     order = np.concatenate([np.arange(0, block, 2), np.arange(1, block, 2)])
     angle = np.pi * np.outer(2 * order + 1, np.arange(block)) / (2 * block)
     parts = np.stack([np.cos(angle), -np.sin(angle)]).reshape(2, GROUPS, block // GROUPS, block)
-    forward = parts.transpose(1, 0, 2, 3).reshape(2 * block, block).astype(jnp.bfloat16)
-    return jnp.asarray(forward), jnp.asarray(forward.T.copy())
+    exact = parts.transpose(1, 0, 2, 3).reshape(2 * block, block)
+    high = exact.astype(jnp.bfloat16)
+    low = (exact - high.astype(np.float64)).astype(jnp.bfloat16)
+    return jnp.asarray(np.concatenate([high, low], axis=1)), jnp.asarray(high.T.copy())
 
 
 def params(flops, moved, limit=16):
@@ -223,14 +225,14 @@
 
 
 def transform(table_ref, spec_ref, group, in_ref, offset, tokens, tile):
-    block = table_ref.shape[1]
+    block = table_ref.shape[1] // 2
     per = block // tokens
     blocks = []
     for b in range(2):
         parts = [
             in_ref[(2 * tile + b) * per + p, offset : offset + tokens, :] for p in range(per)
         ]
-        blocks.append(jnp.concatenate(parts, axis=0))
+        blocks.append(jnp.concatenate(parts + parts, axis=0))
     columns = jnp.concatenate(blocks, axis=1)
     size = spec_ref.shape[0]
     rows = table_ref[group * size : (group + 1) * size, :]
@@ -400,7 +402,7 @@
 def convolve(received, tables, scale):
     pieces, rows, _ = received.shape
     tokens = rows // 2
-    freq, block = tables[0].shape
+    block, freq = tables[1].shape
     wide = pieces * tokens // block * LANES
 
     def kernel(*refs):
@@ -414,13 +416,13 @@
         scratch_shapes=[pltpu.VMEM((freq, wide), jnp.bfloat16)]
         + [pltpu.VMEM((freq // GROUPS, wide), jnp.float32)] * (2 * GROUPS),
         name="forward",
-        **params(6 * freq * block * wide, 8 * freq * wide),
+        **params(10 * freq * block * wide, 8 * freq * wide),
     )(received, *tables)
 
 
 def correlate(grads, received, tables, scale):
     pieces, tokens, _ = grads.shape
-    freq, block = tables[0].shape
+    block, freq = tables[1].shape
     wide = pieces * tokens // block * LANES
 
     def kernel(*refs):
@@ -438,7 +440,7 @@
         + [pltpu.VMEM((freq, wide), jnp.bfloat16)] * 2
         + [pltpu.VMEM((freq // GROUPS, wide), jnp.float32)] * (3 * GROUPS),
         name="backward",
-        **params(10 * freq * block * wide, 8 * freq * wide),
+        **params(16 * freq * block * wide, 8 * freq * wide),
     )(grads, received, *tables)
 
 

time: 113 us -> 114 us (level)
  no operation moved by 1% of the time
where the time goes in v5:
time: 114 us; the launch traced here: 113 us
  blocking collectives  70.5 us (62%)
  waiting for transfers between devices  20.5 us (18%)
  Pallas kernels  15.1 us (13%)
  starting transfers between devices  5.76 us (5%)
    all_to_all x3, blocking collectives, exchange(): lax.all_to_all(pieces, 'ctx', split_axis=0, concat_axis=0, tiled=True)  70.5 us
    all_to_all x1, waiting for transfers between devices, exchange(): lax.all_to_all(pieces, 'ctx', split_axis=0, concat_axis=0, tiled=True)  19.3 us
    pallas_call x1, Pallas kernels, correlate(): pl.pallas_call(kernel, in_specs=whole(4), out_specs=pl.BlockSpec(memory_s...  4.7 us
    all_to_all x1, starting transfers between devices, exchange(): lax.all_to_all(pieces, 'ctx', split_axis=0, concat_axis=0, tiled=True)  4.45 us
    pallas_call x1, Pallas kernels, gate_norm(): pl.pallas_call(kernel, grid=(4,), in_specs=[small, small, wide, wide, pl....  3.89 us
    pallas_call x1, Pallas kernels, pack(): pl.pallas_call(pack_kernel, in_specs=[pl.BlockSpec(memory_space=pltpu.HBM...  2.36 us
  transfers between devices with their start and end apart: 2, of which 2 were waited for; matrix products, arithmetic and copies ran while one was open for 0% of the time, Pallas kernels for 3%

profile of v5, /device:TPU:1, one launch (start us, length us, event | category | flops | bytes accessed | tf_op | source)
XLA Modules:
  0.0 112.7 jit_solution(17243355723310782737)
XLA Ops:
  0.6 2.4 %pack.1 = bf16[16,2,128,128]{3,2,1,0:T(8,128)(2,1)} custom-call(bf16[128,2048]{1,0:T(8,128)(2,1)} %key_ref.1, bf16[128,2048]{1,0:T(8,128)(2,1)} %value_ref.1, bf16[128,2048]{1,0:T(8,128)(2,1)} %taps_hbm.1), custom_call_target="tpu_custom_call" | custom-call | flops 262144 | bytes 2621440 | tf_op jit(solution)/shard_map/pack/pallas_call | solution.py:208
  3.0 0.0 copy-start.7
  3.0 0.0 copy-start.8
  3.0 32.7 %all_to_all.20.refs_0_.refs_1_ = bf16[16,256,128]{2,1,0:T(8,128)(2,1)S(1)} all-to-all(bf16[16,256,128]{2,1,0:T(8,128)(2,1)} %bitcast.1), channel_id=1, replica_groups=mesh['ctx'=16,'tp'=2] {'ctx'}, dimensions={0} | all-to-all | bytes 2097152 | tf_op jit(solution)/shard_map/all_to_all | solution.py:606
  35.7 0.0 copy-done.7
  35.7 2.1 %forward.1 = bf16[16,128,128]{2,1,0:T(8,128)(2,1)S(1)} custom-call(bf16[16,256,128]{2,1,0:T(8,128)(2,1)S(1)} %all_to_all.20.refs_0_.refs_1_, bf16[512,512]{1,0:T(8,128)(2,1)S(1)} %copy-done.7, bf16[256,512]{1,0:T(8,128)(2,1)S(1)} %copy-done.8), custom_call_target="tpu_custom_call" | custom-call | flops 1342177280 | bytes 4194304 | tf_op jit(solution)/shard_map/forward/pallas_call | solution.py:411
  37.8 0.0 copy-start.1
  37.8 0.0 copy-start.2
  37.8 18.4 %all_to_all.21.conv_ref.refs_4_ = bf16[16,128,128]{2,1,0:T(8,128)(2,1)S(1)} all-to-all(bf16[16,128,128]{2,1,0:T(8,128)(2,1)S(1)} %forward.1), channel_id=1, replica_groups=mesh['ctx'=16,'tp'=2] {'ctx'}, dimensions={0} | all-to-all | bytes 1048576 | tf_op jit(solution)/shard_map/all_to_all | solution.py:606
  56.2 0.0 copy-done.1
  56.2 0.4 sums.1.own_ref.refs_0_
  56.6 0.0 copy-start.5
  56.6 1.3 %collective-permute-start = (f32[2,128]{1,0:T(2,128)S(1)}, f32[2,128]{1,0:T(2,128)S(1)}, u32[]{:S(2)}, u32[]{:S(2)}) collective-permute-start(f32[2,128]{1,0:T(2,128)S(1)} %sums.1.own_ref.refs_0_), channel_id=1, source_target_pairs={{0,1},{1,0},{2,3},{3,2},{4,5},{5,4},{6,7},{7,6},{8,9},{9,8},{10,11... | collective-permute-start | bytes 3080 | tf_op jit(solution)/shard_map/ppermute | solution.py:618
  57.9 1.2 %collective-permute-done.other_ref.refs_1_ = f32[2,128]{1,0:T(2,128)S(1)} collective-permute-done((f32[2,128]{1,0:T(2,128)S(1)}, f32[2,128]{1,0:T(2,128)S(1)}, u32[]{:S(2)}, u32[]{:S(2)}) %collective-permute-start) | collective-permute-done | bytes 1056 | tf_op jit(solution)/shard_map/ppermute | solution.py:618
  59.1 0.0 copy-done
  59.1 0.4 gate_grad.1
  59.5 0.2 copy-done.6
  59.6 19.4 %all_to_all.22.refs_0_ = bf16[16,128,128]{2,1,0:T(8,128)(2,1)S(1)} all-to-all(bf16[16,128,128]{2,1,0:T(8,128)(2,1)S(1)} %gate_grad.1), channel_id=1, replica_groups=mesh['ctx'=16,'tp'=2] {'ctx'}, dimensions={0} | all-to-all | bytes 1048576 | tf_op jit(solution)/shard_map/all_to_all | solution.py:606
  79.0 4.7 %backward.1 = bf16[16,256,128]{2,1,0:T(8,128)(2,1)} custom-call(bf16[16,128,128]{2,1,0:T(8,128)(2,1)S(1)} %all_to_all.22.refs_0_, bf16[16,256,128]{2,1,0:T(8,128)(2,1)S(1)} %all_to_all.20.refs_0_.refs_1_, bf16[512,512]{1,0:T(8,128)(2,1)S(1)} %copy-done.7, bf16[256,512]{1,0:T(8,128)(2,1)S(1)} %copy-done.8), custom_call_target="tpu_custom_call" | custom-call | flops 2147483648 | bytes 4194304 | tf_op jit(solution)/shard_map/backward/pallas_call | solution.py:431
  83.7 4.5 %all-to-all-start.3 = ((bf16[16,256,128]{2,1,0:T(8,128)(2,1)}), bf16[16,256,128]{2,1,0:T(8,128)(2,1)S(1)}, u32[]{:S(2)}, u32[]{:S(2)}) async-start(bf16[16,256,128]{2,1,0:T(8,128)(2,1)} %backward.1), calls=%async_computation.3 | async-start | bytes 2097152 | tf_op jit(solution)/shard_map/all_to_all | solution.py:606
  88.2 0.0 copy-start.4
  88.2 3.9 %norm.1 = (bf16[128,2048]{1,0:T(8,128)(2,1)}, bf16[128,2048]{1,0:T(8,128)(2,1)}) custom-call(f32[2,128]{1,0:T(2,128)} %copy-done.5, f32[2,128]{1,0:T(2,128)} %copy-done.6, bf16[128,2048]{1,0:T(8,128)(2,1)} %refs_2_.3, bf16[128,2048]{1,0:T(8,128)(2,1)} %refs_3_.2, bf16[16,128,128]{2,1,0:T(8,128)(2,1)} %copy-done), custom_call_target="tpu_custom_call" | custom-call | flops 1572864 | bytes 2621440 | tf_op jit(solution)/shard_map/norm/pallas_call | solution.py:544
  92.1 19.3 %all-to-all-done.3.back_ref = bf16[16,256,128]{2,1,0:T(8,128)(2,1)S(1)} async-done(((bf16[16,256,128]{2,1,0:T(8,128)(2,1)}), bf16[16,256,128]{2,1,0:T(8,128)(2,1)S(1)}, u32[]{:S(2)}, u32[]{:S(2)}) %all-to-all-start.3) | async-done | bytes 1048608 | tf_op jit(solution)/shard_map/all_to_all | solution.py:606
  111.4 1.3 %unpack.1 = (bf16[128,2048]{1,0:T(8,128)(2,1)}, bf16[128,2048]{1,0:T(8,128)(2,1)}, bf16[128,2048]{1,0:T(8,128)(2,1)}) custom-call(bf16[16,256,128]{2,1,0:T(8,128)(2,1)S(1)} %all-to-all-done.3.back_ref, bf16[128,2048]{1,0:T(8,128)(2,1)S(1)} %copy-done.3, bf16[128,2048]{1,0:T(8,128)(2,1)S(1)} %copy-done.4), custom_call_target="tpu_custom_call" | custom-call | flops 524288 | bytes 3670016 | tf_op jit(solution)/shard_map/unpack/pallas_call | solution.py:589
  (8 shorter events, 0.0 us)
Async XLA Ops:
  3.0 32.7 %copy-start.7 = (bf16[512,512]{1,0:T(8,128)(2,1)S(1)}, bf16[512,512]{1,0:T(8,128)(2,1)}, u32[]{:S(2)}) copy-start(bf16[512,512]{1,0:T(8,128)(2,1)} %constant.4.clone.refs_1_.refs_2_) | copy-start | bytes 1572868
  3.0 32.7 %copy-start.8 = (bf16[256,512]{1,0:T(8,128)(2,1)S(1)}, bf16[256,512]{1,0:T(8,128)(2,1)}, u32[]{:S(2)}) copy-start(bf16[256,512]{1,0:T(8,128)(2,1)} %constant.5.clone.refs_2_.refs_3_) | copy-start | bytes 786436
  37.8 18.4 %copy-start.1 = (bf16[128,2048]{1,0:T(8,128)(2,1)S(1)}, bf16[128,2048]{1,0:T(8,128)(2,1)}, u32[]{:S(2)}) copy-start(bf16[128,2048]{1,0:T(8,128)(2,1)} %refs_2_.3) | copy-start | bytes 1572868
  37.8 18.4 %copy-start.2 = (bf16[128,2048]{1,0:T(8,128)(2,1)S(1)}, bf16[128,2048]{1,0:T(8,128)(2,1)}, u32[]{:S(2)}) copy-start(bf16[128,2048]{1,0:T(8,128)(2,1)} %refs_3_.2) | copy-start | bytes 1572868
  56.2 2.9 %copy-start = (bf16[16,128,128]{2,1,0:T(8,128)(2,1)}, bf16[16,128,128]{2,1,0:T(8,128)(2,1)S(1)}, u32[]{:S(2)}) copy-start(bf16[16,128,128]{2,1,0:T(8,128)(2,1)S(1)} %all_to_all.21.conv_ref.refs_4_) | copy-start | bytes 1572868
  56.6 2.9 %copy-start.5 = (f32[2,128]{1,0:T(2,128)}, f32[2,128]{1,0:T(2,128)S(1)}, u32[]{:S(2)}) copy-start(f32[2,128]{1,0:T(2,128)S(1)} %sums.1.own_ref.refs_0_) | copy-start | bytes 3076
  56.6 2.5 %collective-permute-start = (f32[2,128]{1,0:T(2,128)S(1)}, f32[2,128]{1,0:T(2,128)S(1)}, u32[]{:S(2)}, u32[]{:S(2)}) collective-permute-start(f32[2,128]{1,0:T(2,128)S(1)} %sums.1.own_ref.refs_0_), channel_id=1, source_target_pairs={{0,1},{1,0},{2,3},{3,2},{4,5},{5,4},{6,7},{7,6},{8,9},{9,8},{10,11... | collective-permute-start | bytes 3080 | tf_op jit(solution)/shard_map/ppermute | solution.py:618
  59.1 0.6 copy-start.6
  83.7 27.6 %all-to-all-start.3 = ((bf16[16,256,128]{2,1,0:T(8,128)(2,1)}), bf16[16,256,128]{2,1,0:T(8,128)(2,1)S(1)}, u32[]{:S(2)}, u32[]{:S(2)}) async-start(bf16[16,256,128]{2,1,0:T(8,128)(2,1)} %backward.1), calls=%async_computation.3 | async-start | bytes 2097152 | tf_op jit(solution)/shard_map/all_to_all | solution.py:606
  88.2 23.2 %copy-start.3 = (bf16[128,2048]{1,0:T(8,128)(2,1)S(1)}, bf16[128,2048]{1,0:T(8,128)(2,1)}, u32[]{:S(2)}) copy-start(bf16[128,2048]{1,0:T(8,128)(2,1)} %key_ref.1) | copy-start | bytes 1572868
  88.2 23.2 %copy-start.4 = (bf16[128,2048]{1,0:T(8,128)(2,1)S(1)}, bf16[128,2048]{1,0:T(8,128)(2,1)}, u32[]{:S(2)}) copy-start(bf16[128,2048]{1,0:T(8,128)(2,1)} %value_ref.1) | copy-start | bytes 1572868

commit v6 on v4

--- a/solution.py
+++ b/solution.py
@@ -293,14 +293,14 @@
         before = (real, imag)
 
 
-def backward_products(grad_ref, other_ref, acc_ref, group, row):
+def backward_products(grad_ref, other_ref, acc_ref, group, row, first_block, last_block):
     count = grad_ref.shape[1] // LANES
     others = [tile_of(other_ref, row, b) for b in range(count)]
     others = [(r, i, r - i) for r, i in others]
     grads = [tile_of(grad_ref, row, b) for b in range(count)]
     grads = [(r, i, r + i) for r, i in grads]
     after = None
-    for d in reversed(range(count)):
+    for d in reversed(range(first_block, min(last_block + 1, count))):
         first = second = third = None
         for k in range(count - d):
             gr, gi, gs = grads[d + k]
@@ -310,7 +310,9 @@
             third = plus(third, gs * ad)
         real = first + second
         imag = third - first + second
-        if after is None:
+        if d == last_block:
+            pass
+        elif after is None:
             put_tile(acc_ref, group, row, d, real, imag)
         elif group < GROUPS // 2:
             put_tile(acc_ref, group, row, d, real + after[1], imag - after[0])
@@ -377,20 +379,27 @@
             if group + 1 < GROUPS:
                 transforms(group + 1, i)
             transform(table_ref, mixes[group], group, in_ref, 0, tokens, i)
-            backward_products(grads[group], taps[group], mixed_ref, group, row)
+            backward_products(grads[group], taps[group], mixed_ref, group, row, 0, 2 * tiles)
 
         each_step(tiles, step)
-    for group in range(GROUPS):
-
-        def step(i, group=group):
-            row = i * ROWS
-            if i == 0:
-                restore(back_ref, mixed_ref, out_ref, 0, tokens, scale, group)
-                send(0, 0, group)
-            backward_products(grads[group], mixes[group], dtaps_ref, group, row)
-
-        each_step(tiles, step)
-    for tile in range(tiles):
+    for upper in (True, False):
+        first_block, last_block = (tiles, 2 * tiles) if upper else (0, tiles)
+        for group in range(GROUPS):
+
+            def step(i, group=group, upper=upper, first_block=first_block, last_block=last_block):
+                row = i * ROWS
+                if i == 0 and upper:
+                    restore(back_ref, mixed_ref, out_ref, 0, tokens, scale, group)
+                    send(0, 0, group)
+                if i == 0 and not upper and group < tiles // 2:
+                    restore(back_ref, dtaps_ref, out_ref, tokens, tokens, scale, tiles // 2 + group)
+                    send(tokens, 1, tiles // 2 + group)
+                backward_products(
+                    grads[group], mixes[group], dtaps_ref, group, row, first_block, last_block
+                )
+
+            each_step(tiles, step)
+    for tile in range(tiles // 2):
         restore(back_ref, dtaps_ref, out_ref, tokens, tokens, scale, tile)
         send(tokens, 1, tile)
     for copy in copies:

time: 113 us -> 113 us (level)
  no operation moved by 1% of the time
where the time goes in v6:
time: 113 us; the launch traced here: 112 us
  blocking collectives  70.5 us (62%)
  waiting for transfers between devices  20.5 us (18%)
  Pallas kernels  14.4 us (13%)
  starting transfers between devices  5.75 us (5%)
    all_to_all x3, blocking collectives, exchange(): lax.all_to_all(pieces, 'ctx', split_axis=0, concat_axis=0, tiled=True)  70.5 us
    all_to_all x1, waiting for transfers between devices, exchange(): lax.all_to_all(pieces, 'ctx', split_axis=0, concat_axis=0, tiled=True)  19.3 us
    all_to_all x1, starting transfers between devices, exchange(): lax.all_to_all(pieces, 'ctx', split_axis=0, concat_axis=0, tiled=True)  4.45 us
    pallas_call x1, Pallas kernels, correlate(): pl.pallas_call(kernel, in_specs=whole(4), out_specs=pl.BlockSpec(memory_s...  4.25 us
    pallas_call x1, Pallas kernels, gate_norm(): pl.pallas_call(kernel, grid=(4,), in_specs=[small, small, wide, wide, pl....  3.89 us
    pallas_call x1, Pallas kernels, pack(): pl.pallas_call(pack_kernel, in_specs=[pl.BlockSpec(memory_space=pltpu.HBM...  2.36 us
  transfers between devices with their start and end apart: 2, of which 2 were waited for; matrix products, arithmetic and copies ran while one was open for 0% of the time, Pallas kernels for 3%

profile of v6, /device:TPU:1, one launch (start us, length us, event | category | flops | bytes accessed | tf_op | source)
XLA Modules:
  0.0 112.0 jit_solution(9319687943601559131)
XLA Ops:
  0.6 2.4 %pack.1 = bf16[16,2,128,128]{3,2,1,0:T(8,128)(2,1)} custom-call(bf16[128,2048]{1,0:T(8,128)(2,1)} %key_ref.1, bf16[128,2048]{1,0:T(8,128)(2,1)} %value_ref.1, bf16[128,2048]{1,0:T(8,128)(2,1)} %taps_hbm.1), custom_call_target="tpu_custom_call" | custom-call | flops 262144 | bytes 2621440 | tf_op jit(solution)/shard_map/pack/pallas_call | solution.py:206
  3.0 0.0 copy-start.7
  3.0 0.0 copy-start.8
  3.0 32.7 %all_to_all.20.refs_0_.refs_1_ = bf16[16,256,128]{2,1,0:T(8,128)(2,1)S(1)} all-to-all(bf16[16,256,128]{2,1,0:T(8,128)(2,1)} %bitcast.1), channel_id=1, replica_groups=mesh['ctx'=16,'tp'=2] {'ctx'}, dimensions={0} | all-to-all | bytes 2097152 | tf_op jit(solution)/shard_map/all_to_all | solution.py:613
  35.7 1.8 %forward.1 = bf16[16,128,128]{2,1,0:T(8,128)(2,1)S(1)} custom-call(bf16[16,256,128]{2,1,0:T(8,128)(2,1)S(1)} %all_to_all.20.refs_0_.refs_1_, bf16[512,256]{1,0:T(8,128)(2,1)S(1)} %copy-done.7, bf16[256,512]{1,0:T(8,128)(2,1)S(1)} %copy-done.8), custom_call_target="tpu_custom_call" | custom-call | flops 805306368 | bytes 4194304 | tf_op jit(solution)/shard_map/forward/pallas_call | solution.py:418
  37.6 0.0 copy-start.1
  37.6 0.0 copy-start.2
  37.6 18.4 %all_to_all.21.conv_ref.refs_4_ = bf16[16,128,128]{2,1,0:T(8,128)(2,1)S(1)} all-to-all(bf16[16,128,128]{2,1,0:T(8,128)(2,1)S(1)} %forward.1), channel_id=1, replica_groups=mesh['ctx'=16,'tp'=2] {'ctx'}, dimensions={0} | all-to-all | bytes 1048576 | tf_op jit(solution)/shard_map/all_to_all | solution.py:613
  56.0 0.0 copy-done.1
  56.0 0.4 sums.1.own_ref.refs_0_
  56.4 0.0 copy-start.5
  56.4 1.3 %collective-permute-start = (f32[2,128]{1,0:T(2,128)S(1)}, f32[2,128]{1,0:T(2,128)S(1)}, u32[]{:S(2)}, u32[]{:S(2)}) collective-permute-start(f32[2,128]{1,0:T(2,128)S(1)} %sums.1.own_ref.refs_0_), channel_id=1, source_target_pairs={{0,1},{1,0},{2,3},{3,2},{4,5},{5,4},{6,7},{7,6},{8,9},{9,8},{10,11... | collective-permute-start | bytes 3080 | tf_op jit(solution)/shard_map/ppermute | solution.py:625
  57.7 1.2 %collective-permute-done.other_ref.refs_1_ = f32[2,128]{1,0:T(2,128)S(1)} collective-permute-done((f32[2,128]{1,0:T(2,128)S(1)}, f32[2,128]{1,0:T(2,128)S(1)}, u32[]{:S(2)}, u32[]{:S(2)}) %collective-permute-start) | collective-permute-done | bytes 1056 | tf_op jit(solution)/shard_map/ppermute | solution.py:625
  58.9 0.0 copy-done
  58.9 0.4 gate_grad.1
  59.2 0.2 copy-done.6
  59.4 19.4 %all_to_all.22.refs_0_ = bf16[16,128,128]{2,1,0:T(8,128)(2,1)S(1)} all-to-all(bf16[16,128,128]{2,1,0:T(8,128)(2,1)S(1)} %gate_grad.1), channel_id=1, replica_groups=mesh['ctx'=16,'tp'=2] {'ctx'}, dimensions={0} | all-to-all | bytes 1048576 | tf_op jit(solution)/shard_map/all_to_all | solution.py:613
  78.8 4.2 %backward.1 = bf16[16,256,128]{2,1,0:T(8,128)(2,1)} custom-call(bf16[16,128,128]{2,1,0:T(8,128)(2,1)S(1)} %all_to_all.22.refs_0_, bf16[16,256,128]{2,1,0:T(8,128)(2,1)S(1)} %all_to_all.20.refs_0_.refs_1_, bf16[512,256]{1,0:T(8,128)(2,1)S(1)} %copy-done.7, bf16[256,512]{1,0:T(8,128)(2,1)S(1)} %copy-done.8), custom_call_target="tpu_custom_call" | custom-call | flops 1342177280 | bytes 4194304 | tf_op jit(solution)/shard_map/backward/pallas_call | solution.py:438
  83.1 4.5 %all-to-all-start.3 = ((bf16[16,256,128]{2,1,0:T(8,128)(2,1)}), bf16[16,256,128]{2,1,0:T(8,128)(2,1)S(1)}, u32[]{:S(2)}, u32[]{:S(2)}) async-start(bf16[16,256,128]{2,1,0:T(8,128)(2,1)} %backward.1), calls=%async_computation.3 | async-start | bytes 2097152 | tf_op jit(solution)/shard_map/all_to_all | solution.py:613
  87.5 0.0 copy-start.4
  87.5 3.9 %norm.1 = (bf16[128,2048]{1,0:T(8,128)(2,1)}, bf16[128,2048]{1,0:T(8,128)(2,1)}) custom-call(f32[2,128]{1,0:T(2,128)} %copy-done.5, f32[2,128]{1,0:T(2,128)} %copy-done.6, bf16[128,2048]{1,0:T(8,128)(2,1)} %refs_2_.3, bf16[128,2048]{1,0:T(8,128)(2,1)} %refs_3_.2, bf16[16,128,128]{2,1,0:T(8,128)(2,1)} %copy-done), custom_call_target="tpu_custom_call" | custom-call | flops 1572864 | bytes 2621440 | tf_op jit(solution)/shard_map/norm/pallas_call | solution.py:551
  91.4 19.3 %all-to-all-done.3.back_ref = bf16[16,256,128]{2,1,0:T(8,128)(2,1)S(1)} async-done(((bf16[16,256,128]{2,1,0:T(8,128)(2,1)}), bf16[16,256,128]{2,1,0:T(8,128)(2,1)S(1)}, u32[]{:S(2)}, u32[]{:S(2)}) %all-to-all-start.3) | async-done | bytes 1048608 | tf_op jit(solution)/shard_map/all_to_all | solution.py:613
  110.7 0.0 copy-done.3
  110.7 1.3 %unpack.1 = (bf16[128,2048]{1,0:T(8,128)(2,1)}, bf16[128,2048]{1,0:T(8,128)(2,1)}, bf16[128,2048]{1,0:T(8,128)(2,1)}) custom-call(bf16[16,256,128]{2,1,0:T(8,128)(2,1)S(1)} %all-to-all-done.3.back_ref, bf16[128,2048]{1,0:T(8,128)(2,1)S(1)} %copy-done.3, bf16[128,2048]{1,0:T(8,128)(2,1)S(1)} %copy-done.4), custom_call_target="tpu_custom_call" | custom-call | flops 524288 | bytes 3670016 | tf_op jit(solution)/shard_map/unpack/pallas_call | solution.py:596
  (8 shorter events, 0.0 us)
Async XLA Ops:
  3.0 32.7 %copy-start.7 = (bf16[512,256]{1,0:T(8,128)(2,1)S(1)}, bf16[512,256]{1,0:T(8,128)(2,1)}, u32[]{:S(2)}) copy-start(bf16[512,256]{1,0:T(8,128)(2,1)} %constant.4.clone.refs_1_.refs_2_) | copy-start | bytes 786436
  3.0 32.7 %copy-start.8 = (bf16[256,512]{1,0:T(8,128)(2,1)S(1)}, bf16[256,512]{1,0:T(8,128)(2,1)}, u32[]{:S(2)}) copy-start(bf16[256,512]{1,0:T(8,128)(2,1)} %constant.5.clone.refs_2_.refs_3_) | copy-start | bytes 786436
  37.6 18.4 %copy-start.1 = (bf16[128,2048]{1,0:T(8,128)(2,1)S(1)}, bf16[128,2048]{1,0:T(8,128)(2,1)}, u32[]{:S(2)}) copy-start(bf16[128,2048]{1,0:T(8,128)(2,1)} %refs_2_.3) | copy-start | bytes 1572868
  37.6 18.4 %copy-start.2 = (bf16[128,2048]{1,0:T(8,128)(2,1)S(1)}, bf16[128,2048]{1,0:T(8,128)(2,1)}, u32[]{:S(2)}) copy-start(bf16[128,2048]{1,0:T(8,128)(2,1)} %refs_3_.2) | copy-start | bytes 1572868
  56.0 2.9 %copy-start = (bf16[16,128,128]{2,1,0:T(8,128)(2,1)}, bf16[16,128,128]{2,1,0:T(8,128)(2,1)S(1)}, u32[]{:S(2)}) copy-start(bf16[16,128,128]{2,1,0:T(8,128)(2,1)S(1)} %all_to_all.21.conv_ref.refs_4_) | copy-start | bytes 1572868
  56.4 2.9 %copy-start.5 = (f32[2,128]{1,0:T(2,128)}, f32[2,128]{1,0:T(2,128)S(1)}, u32[]{:S(2)}) copy-start(f32[2,128]{1,0:T(2,128)S(1)} %sums.1.own_ref.refs_0_) | copy-start | bytes 3076
  56.4 2.5 %collective-permute-start = (f32[2,128]{1,0:T(2,128)S(1)}, f32[2,128]{1,0:T(2,128)S(1)}, u32[]{:S(2)}, u32[]{:S(2)}) collective-permute-start(f32[2,128]{1,0:T(2,128)S(1)} %sums.1.own_ref.refs_0_), channel_id=1, source_target_pairs={{0,1},{1,0},{2,3},{3,2},{4,5},{5,4},{6,7},{7,6},{8,9},{9,8},{10,11... | collective-permute-start | bytes 3080 | tf_op jit(solution)/shard_map/ppermute | solution.py:625
  58.9 0.6 copy-start.6
  83.1 27.6 %all-to-all-start.3 = ((bf16[16,256,128]{2,1,0:T(8,128)(2,1)}), bf16[16,256,128]{2,1,0:T(8,128)(2,1)S(1)}, u32[]{:S(2)}, u32[]{:S(2)}) async-start(bf16[16,256,128]{2,1,0:T(8,128)(2,1)} %backward.1), calls=%async_computation.3 | async-start | bytes 2097152 | tf_op jit(solution)/shard_map/all_to_all | solution.py:613
  87.5 23.2 %copy-start.3 = (bf16[128,2048]{1,0:T(8,128)(2,1)S(1)}, bf16[128,2048]{1,0:T(8,128)(2,1)}, u32[]{:S(2)}) copy-start(bf16[128,2048]{1,0:T(8,128)(2,1)} %key_ref.1) | copy-start | bytes 1572868
  87.5 23.2 %copy-start.4 = (bf16[128,2048]{1,0:T(8,128)(2,1)S(1)}, bf16[128,2048]{1,0:T(8,128)(2,1)}, u32[]{:S(2)}) copy-start(bf16[128,2048]{1,0:T(8,128)(2,1)} %value_ref.1) | copy-start | bytes 1572868
